TPU v7x, 32 devices: a whole 2x2x4 slice. The times are simulated.
32 devices in a mesh: dp: 2 (over y), fsdp: 16 (over z, x, core).
Axes of the slice: x: 2, y: 2, z: 4, core: 2. Of those that a mesh axis runs over, the one named last changes fastest.
Arguments:
- tokens: bfloat16 [32768, 768], P(('dp', 'fsdp')), may hold values from -6 to 6
- segment_ids: int32 [32, 1024], P(('dp', 'fsdp')), may hold values from 0 to 7, never falling along the last dimension, each value on 1 to 512 neighbouring positions
- padding: int32 [32, 1024], P(('dp', 'fsdp')), may hold values 0 or 1
- qkv_weight: bfloat16 [768, 2304], P(None, 'fsdp'), may hold values from -0.21875 to 0.21875
- query_bias: bfloat16 [768], P('fsdp'), may hold values from -1.25 to 1.25
- value_bias: bfloat16 [768], P('fsdp'), may hold values from -1.25 to 1.25
- out_weight: bfloat16 [768, 768], P('fsdp'), may hold values from -0.875 to 0.875
- out_bias: bfloat16 [768], P('fsdp'), may hold values from -1.25 to 1.25
- first_gain: bfloat16 [768], P('fsdp'), may hold values from 0.5 to 1.5
- first_shift: bfloat16 [768], P('fsdp'), may hold values from -1.25 to 1.25
- second_gain: bfloat16 [768], P('fsdp'), may hold values from 0.5 to 1.5
- second_shift: bfloat16 [768], P('fsdp'), may hold values from -1.25 to 1.25
- up_weight: bfloat16 [768, 3072], P(None, 'fsdp'), may hold values from -0.21875 to 0.21875
- up_bias: bfloat16 [3072], P('fsdp'), may hold values from -1.25 to 1.25
- down_weight: bfloat16 [3072, 768], P('fsdp'), may hold values from -0.109375 to 0.109375
- down_bias: bfloat16 [768], P('fsdp'), may hold values from -1.25 to 1.25
- align_weight: bfloat16 [768, 1024], P(None, 'fsdp'), may hold values from -0.21875 to 0.21875
- align_bias: bfloat16 [1024], P('fsdp'), may hold values from -1.25 to 1.25
- grad_output: bfloat16 [32768, 768], P(('dp', 'fsdp')), may hold values from -12 to 12
- grad_aligned: bfloat16 [32768, 1024], P(('dp', 'fsdp')), may hold values from -6 to 6
Outputs:
- block_out: bfloat16 [32768, 768], P(('dp', 'fsdp'))
- aligned: bfloat16 [32768, 1024], P(('dp', 'fsdp'))
- grad_tokens: bfloat16 [32768, 768], P(('dp', 'fsdp'))
- grad_qkv_weight: float32 [768, 2304], P(None, 'fsdp')
- grad_query_bias: float32 [768], P('fsdp')
- grad_value_bias: float32 [768], P('fsdp')
- grad_out_weight: float32 [768, 768], P('fsdp')
- grad_out_bias: float32 [768], P('fsdp')
- grad_first_gain: float32 [768], P('fsdp')
- grad_first_shift: float32 [768], P('fsdp')
- grad_second_gain: float32 [768], P('fsdp')
- grad_second_shift: float32 [768], P('fsdp')
- grad_up_weight: float32 [768, 3072], P(None, 'fsdp')
- grad_up_bias: float32 [3072], P('fsdp')
- grad_down_weight: float32 [3072, 768], P('fsdp')
- grad_down_bias: float32 [768], P('fsdp')
- grad_align_weight: float32 [768, 1024], P(None, 'fsdp')
- grad_align_bias: float32 [1024], P('fsdp')
Inputs may be any that keep to these rules, and one draw needn't show every extreme that they name: `segment_ids`: segment numbers never fall along a packed sequence; each clip holds at most 512 tokens.
All inputs are finite; a program needn't handle non-finite values. No bound on the sum of `padding` on one device may be relied on, other than what follows from the above.
Results may differ from a plain program's by a relative error of at most 0.014.
Values may be sent and summed in bfloat16 or wider, within the bound.
A program may use at most 256 MiB of HBM per device.

v0:
```python
import math

import jax
import jax.numpy as jnp
from jax import lax
from jax.sharding import PartitionSpec as P

HEADS = 12


def layer_norm(values, norm_gain, norm_shift):
    row_mean = jnp.mean(values, -1, keepdims=True)
    centered = values - row_mean
    variance = jnp.mean(centered * centered, -1, keepdims=True)
    return centered * lax.rsqrt(variance + 1e-05) * norm_gain + norm_shift


def gelu_exact(values):
    return jax.nn.gelu(values, approximate=False)


def product(left, right):
    return jnp.dot(left, right, preferred_element_type=jnp.float32)


def product_right_t(left, right):
    return lax.dot_general(
        left, right, (((1,), (1,)), ((), ())), preferred_element_type=jnp.float32
    )


def outer_sum(left, right):
    return lax.dot_general(
        left, right, (((0,), (0,)), ((), ())), preferred_element_type=jnp.float32
    )


def column_sum(values):
    return jnp.sum(values.astype(jnp.float32), 0)


def block_mask(segment, is_valid, row_start, block_rows):
    length = segment.shape[0]
    row_ids = row_start + jnp.arange(block_rows, dtype=jnp.int32)
    key_ids = jnp.arange(length, dtype=jnp.int32)
    seg_rows = lax.dynamic_slice_in_dim(segment, row_start, block_rows)
    return (seg_rows[:, None] == segment[None, :]) & (
        (is_valid[None, :] > 0.5) | (row_ids[:, None] == key_ids[None, :])
    )


def masked_scores(query_part, key_part, keep_mask, scale):
    scores = (
        jnp.einsum("qhd,khd->hqk", query_part, key_part, preferred_element_type=jnp.float32) * scale
    )
    return jnp.where(keep_mask[None], scores, -1e30)


def attention_forward(query3, key3, value3, segment, is_valid):
    length, head_count, head_size = query3.shape
    block_rows = min(512, length)
    block_count = length // block_rows
    group_size = math.gcd(head_count, 4)
    scale = 1.0 / math.sqrt(head_size)
    starts = jnp.arange(block_count, dtype=jnp.int32) * block_rows
    query_blocks = query3.reshape(block_count, block_rows, head_count, head_size)

    def one_block(block_item):
        query_block, row_start = block_item
        keep_mask = block_mask(segment, is_valid, row_start, block_rows)
        out_parts = []
        lse_parts = []
        for head_first in range(0, head_count, group_size):
            head_slice = slice(head_first, head_first + group_size)
            scores = masked_scores(
                query_block[:, head_slice], key3[:, head_slice], keep_mask, scale
            )
            row_max = jnp.max(scores, -1, keepdims=True)
            row_lse = jnp.log(jnp.sum(jnp.exp(scores - row_max), -1, keepdims=True)) + row_max
            attn_probs = jnp.exp(scores - row_lse).astype(jnp.bfloat16)
            out_parts.append(
                jnp.einsum(
                    "hqk,khd->qhd",
                    attn_probs,
                    value3[:, head_slice],
                    preferred_element_type=jnp.float32,
                )
            )
            lse_parts.append(row_lse[:, :, 0])
        return (jnp.concatenate(out_parts, 1), jnp.concatenate(lse_parts, 0))

    mixed, lse_all = lax.map(one_block, (query_blocks, starts))
    return (mixed.reshape(length, head_count * head_size), lse_all)


def attention_backward(query3, key3, value3, grad3, lse_all, segment, is_valid):
    length, head_count, head_size = query3.shape
    block_rows = min(512, length)
    block_count = length // block_rows
    group_size = math.gcd(head_count, 4)
    scale = 1.0 / math.sqrt(head_size)
    starts = jnp.arange(block_count, dtype=jnp.int32) * block_rows
    query_blocks = query3.reshape(block_count, block_rows, head_count, head_size)
    grad_blocks = grad3.reshape(block_count, block_rows, head_count, head_size)

    def one_block(carry, block_item):
        grad_key, grad_value = carry
        query_block, grad_block, lse_block, row_start = block_item
        keep_mask = block_mask(segment, is_valid, row_start, block_rows)
        query_parts = []
        key_parts = []
        value_parts = []
        for head_first in range(0, head_count, group_size):
            head_slice = slice(head_first, head_first + group_size)
            scores = masked_scores(
                query_block[:, head_slice], key3[:, head_slice], keep_mask, scale
            )
            attn_probs = jnp.exp(scores - lse_block[head_slice][:, :, None])
            grad_probs = jnp.einsum(
                "qhd,khd->hqk",
                grad_block[:, head_slice],
                value3[:, head_slice],
                preferred_element_type=jnp.float32,
            )
            row_dot = jnp.sum(attn_probs * grad_probs, -1, keepdims=True)
            grad_scores = (attn_probs * (grad_probs - row_dot)).astype(jnp.bfloat16)
            query_parts.append(
                jnp.einsum(
                    "hqk,khd->qhd",
                    grad_scores,
                    key3[:, head_slice],
                    preferred_element_type=jnp.float32,
                )
                * scale
            )
            key_parts.append(
                jnp.einsum(
                    "hqk,qhd->khd",
                    grad_scores,
                    query_block[:, head_slice],
                    preferred_element_type=jnp.float32,
                )
                * scale
            )
            value_parts.append(
                jnp.einsum(
                    "hqk,qhd->khd",
                    attn_probs.astype(jnp.bfloat16),
                    grad_block[:, head_slice],
                    preferred_element_type=jnp.float32,
                )
            )
        new_carry = (
            grad_key + jnp.concatenate(key_parts, 1),
            grad_value + jnp.concatenate(value_parts, 1),
        )
        return (new_carry, jnp.concatenate(query_parts, 1))

    zeros_heads = jnp.zeros((length, head_count, head_size), jnp.float32)
    (grad_key, grad_value), grad_query = lax.scan(
        one_block, (zeros_heads, zeros_heads), (query_blocks, grad_blocks, lse_all, starts)
    )
    width_all = head_count * head_size
    return (
        grad_query.reshape(length, width_all),
        grad_key.reshape(length, width_all),
        grad_value.reshape(length, width_all),
    )


def per_device(
    tokens,
    segment_ids,
    padding,
    qkv_weight,
    query_bias,
    value_bias,
    out_weight,
    out_bias,
    first_gain,
    first_shift,
    second_gain,
    second_shift,
    up_weight,
    up_bias,
    down_weight,
    down_bias,
    align_weight,
    align_bias,
    grad_output,
    grad_aligned,
):
    full_set = (
        lax.all_gather(qkv_weight, "fsdp", axis=1, tiled=True),
        lax.all_gather(query_bias, "fsdp", axis=0, tiled=True),
        lax.all_gather(value_bias, "fsdp", axis=0, tiled=True),
        lax.all_gather(out_weight, "fsdp", axis=0, tiled=True),
        lax.all_gather(out_bias, "fsdp", axis=0, tiled=True),
        lax.all_gather(first_gain, "fsdp", axis=0, tiled=True),
        lax.all_gather(first_shift, "fsdp", axis=0, tiled=True),
        lax.all_gather(second_gain, "fsdp", axis=0, tiled=True),
        lax.all_gather(second_shift, "fsdp", axis=0, tiled=True),
        lax.all_gather(up_weight, "fsdp", axis=1, tiled=True),
        lax.all_gather(up_bias, "fsdp", axis=0, tiled=True),
        lax.all_gather(down_weight, "fsdp", axis=0, tiled=True),
        lax.all_gather(down_bias, "fsdp", axis=0, tiled=True),
        lax.all_gather(align_weight, "fsdp", axis=1, tiled=True),
        lax.all_gather(align_bias, "fsdp", axis=0, tiled=True),
    )
    (
        qkv_full,
        query_shift,
        value_shift,
        out_full,
        out_shift,
        gain_first,
        shift_first,
        gain_second,
        shift_second,
        up_full,
        up_shift,
        down_full,
        down_shift,
        align_full,
        align_shift,
    ) = full_set
    length, model_width = tokens.shape
    head_count = HEADS
    head_size = model_width // head_count
    segment = segment_ids[0]
    is_valid = 1.0 - padding[0].astype(jnp.float32)
    inputs = tokens.astype(jnp.float32)
    normed_one, pull_one = jax.vjp(
        layer_norm, inputs, gain_first.astype(jnp.float32), shift_first.astype(jnp.float32)
    )
    normed_low = normed_one.astype(jnp.bfloat16)
    qkv_out = product(normed_low, qkv_full)
    query = (qkv_out[:, :model_width] + query_shift.astype(jnp.float32)).astype(jnp.bfloat16)
    keys = qkv_out[:, model_width : 2 * model_width].astype(jnp.bfloat16)
    values_low = (qkv_out[:, 2 * model_width :] + value_shift.astype(jnp.float32)).astype(
        jnp.bfloat16
    )
    head_shape = (length, head_count, head_size)
    query3 = query.reshape(head_shape)
    key3 = keys.reshape(head_shape)
    value3 = values_low.reshape(head_shape)
    mixed, lse_all = attention_forward(query3, key3, value3, segment, is_valid)
    mixed_low = mixed.astype(jnp.bfloat16)
    resid = inputs + product(mixed_low, out_full) + out_shift.astype(jnp.float32)
    normed_two, pull_two = jax.vjp(
        layer_norm, resid, gain_second.astype(jnp.float32), shift_second.astype(jnp.float32)
    )
    normed_two_low = normed_two.astype(jnp.bfloat16)
    upper = product(normed_two_low, up_full) + up_shift.astype(jnp.float32)
    active, pull_gelu = jax.vjp(gelu_exact, upper)
    active_low = active.astype(jnp.bfloat16)
    branch = product(active_low, down_full) + down_shift.astype(jnp.float32)
    out_low = (is_valid[:, None] * (resid + branch)).astype(jnp.bfloat16)
    aligned = (product(out_low, align_full) + align_shift.astype(jnp.float32)).astype(jnp.bfloat16)
    back_set = (
        lax.all_gather(qkv_weight, "fsdp", axis=1, tiled=True),
        lax.all_gather(query_bias, "fsdp", axis=0, tiled=True),
        lax.all_gather(value_bias, "fsdp", axis=0, tiled=True),
        lax.all_gather(out_weight, "fsdp", axis=0, tiled=True),
        lax.all_gather(out_bias, "fsdp", axis=0, tiled=True),
        lax.all_gather(first_gain, "fsdp", axis=0, tiled=True),
        lax.all_gather(first_shift, "fsdp", axis=0, tiled=True),
        lax.all_gather(second_gain, "fsdp", axis=0, tiled=True),
        lax.all_gather(second_shift, "fsdp", axis=0, tiled=True),
        lax.all_gather(up_weight, "fsdp", axis=1, tiled=True),
        lax.all_gather(up_bias, "fsdp", axis=0, tiled=True),
        lax.all_gather(down_weight, "fsdp", axis=0, tiled=True),
        lax.all_gather(down_bias, "fsdp", axis=0, tiled=True),
        lax.all_gather(align_weight, "fsdp", axis=1, tiled=True),
        lax.all_gather(align_bias, "fsdp", axis=0, tiled=True),
    )
    qkv_back = back_set[0]
    out_back = back_set[3]
    up_back = back_set[9]
    down_back = back_set[11]
    align_back = back_set[13]
    grad_align_w = outer_sum(out_low, grad_aligned)
    grad_align_b = column_sum(grad_aligned)
    grad_block = is_valid[:, None] * (
        grad_output.astype(jnp.float32) + product_right_t(grad_aligned, align_back)
    )
    grad_branch = grad_block.astype(jnp.bfloat16)
    grad_down_w = outer_sum(active_low, grad_branch)
    grad_down_b = column_sum(grad_branch)
    grad_active = product_right_t(grad_branch, down_back)
    grad_upper = pull_gelu(grad_active)[0].astype(jnp.bfloat16)
    grad_up_w = outer_sum(normed_two_low, grad_upper)
    grad_up_b = column_sum(grad_upper)
    grad_normed_two = product_right_t(grad_upper, up_back)
    grad_resid_norm, grad_gain_two, grad_shift_two = pull_two(grad_normed_two)
    grad_resid = grad_block + grad_resid_norm
    grad_attn = grad_resid.astype(jnp.bfloat16)
    grad_out_w = outer_sum(mixed_low, grad_attn)
    grad_out_b = column_sum(grad_attn)
    grad_mixed = product_right_t(grad_attn, out_back).astype(jnp.bfloat16)
    grad_query, grad_key, grad_value = attention_backward(
        query3, key3, value3, grad_mixed.reshape(head_shape), lse_all, segment, is_valid
    )
    grad_query_low = grad_query.astype(jnp.bfloat16)
    grad_value_low = grad_value.astype(jnp.bfloat16)
    grad_qkv = jnp.concatenate([grad_query_low, grad_key.astype(jnp.bfloat16), grad_value_low], 1)
    grad_qkv_w = outer_sum(normed_low, grad_qkv)
    grad_query_b = column_sum(grad_query_low)
    grad_value_b = column_sum(grad_value_low)
    grad_normed_one = product_right_t(grad_qkv, qkv_back)
    grad_input_norm, grad_gain_one, grad_shift_one = pull_one(grad_normed_one)
    grad_tokens = (grad_resid + grad_input_norm).astype(jnp.bfloat16)
    grad_terms = (
        grad_qkv_w,
        grad_query_b,
        grad_value_b,
        grad_out_w,
        grad_out_b,
        grad_gain_one,
        grad_shift_one,
        grad_gain_two,
        grad_shift_two,
        grad_up_w,
        grad_up_b,
        grad_down_w,
        grad_down_b,
        grad_align_w,
        grad_align_b,
    )
    owned = (
        lax.psum_scatter(grad_terms[0], "fsdp", scatter_dimension=1, tiled=True),
        lax.psum_scatter(grad_terms[1], "fsdp", scatter_dimension=0, tiled=True),
        lax.psum_scatter(grad_terms[2], "fsdp", scatter_dimension=0, tiled=True),
        lax.psum_scatter(grad_terms[3], "fsdp", scatter_dimension=0, tiled=True),
        lax.psum_scatter(grad_terms[4], "fsdp", scatter_dimension=0, tiled=True),
        lax.psum_scatter(grad_terms[5], "fsdp", scatter_dimension=0, tiled=True),
        lax.psum_scatter(grad_terms[6], "fsdp", scatter_dimension=0, tiled=True),
        lax.psum_scatter(grad_terms[7], "fsdp", scatter_dimension=0, tiled=True),
        lax.psum_scatter(grad_terms[8], "fsdp", scatter_dimension=0, tiled=True),
        lax.psum_scatter(grad_terms[9], "fsdp", scatter_dimension=1, tiled=True),
        lax.psum_scatter(grad_terms[10], "fsdp", scatter_dimension=0, tiled=True),
        lax.psum_scatter(grad_terms[11], "fsdp", scatter_dimension=0, tiled=True),
        lax.psum_scatter(grad_terms[12], "fsdp", scatter_dimension=0, tiled=True),
        lax.psum_scatter(grad_terms[13], "fsdp", scatter_dimension=1, tiled=True),
        lax.psum_scatter(grad_terms[14], "fsdp", scatter_dimension=0, tiled=True),
    )
    summed = (
        lax.psum(owned[0].astype(jnp.bfloat16), "dp").astype(jnp.float32),
        lax.psum(owned[1].astype(jnp.bfloat16), "dp").astype(jnp.float32),
        lax.psum(owned[2].astype(jnp.bfloat16), "dp").astype(jnp.float32),
        lax.psum(owned[3].astype(jnp.bfloat16), "dp").astype(jnp.float32),
        lax.psum(owned[4].astype(jnp.bfloat16), "dp").astype(jnp.float32),
        lax.psum(owned[5].astype(jnp.bfloat16), "dp").astype(jnp.float32),
        lax.psum(owned[6].astype(jnp.bfloat16), "dp").astype(jnp.float32),
        lax.psum(owned[7].astype(jnp.bfloat16), "dp").astype(jnp.float32),
        lax.psum(owned[8].astype(jnp.bfloat16), "dp").astype(jnp.float32),
        lax.psum(owned[9].astype(jnp.bfloat16), "dp").astype(jnp.float32),
        lax.psum(owned[10].astype(jnp.bfloat16), "dp").astype(jnp.float32),
        lax.psum(owned[11].astype(jnp.bfloat16), "dp").astype(jnp.float32),
        lax.psum(owned[12].astype(jnp.bfloat16), "dp").astype(jnp.float32),
        lax.psum(owned[13].astype(jnp.bfloat16), "dp").astype(jnp.float32),
        lax.psum(owned[14].astype(jnp.bfloat16), "dp").astype(jnp.float32),
    )
    return (
        out_low,
        aligned,
        grad_tokens,
        summed[0],
        summed[1],
        summed[2],
        summed[3],
        summed[4],
        summed[5],
        summed[6],
        summed[7],
        summed[8],
        summed[9],
        summed[10],
        summed[11],
        summed[12],
        summed[13],
        summed[14],
    )


def solution(mesh):
    in_specs = (
        P(("dp", "fsdp"), None),
        P(("dp", "fsdp"), None),
        P(("dp", "fsdp"), None),
        P(None, "fsdp"),
        P("fsdp"),
        P("fsdp"),
        P("fsdp", None),
        P("fsdp"),
        P("fsdp"),
        P("fsdp"),
        P("fsdp"),
        P("fsdp"),
        P(None, "fsdp"),
        P("fsdp"),
        P("fsdp", None),
        P("fsdp"),
        P(None, "fsdp"),
        P("fsdp"),
        P(("dp", "fsdp"), None),
        P(("dp", "fsdp"), None),
    )
    out_specs = (
        P(("dp", "fsdp"), None),
        P(("dp", "fsdp"), None),
        P(("dp", "fsdp"), None),
        P(None, "fsdp"),
        P("fsdp"),
        P("fsdp"),
        P("fsdp", None),
        P("fsdp"),
        P("fsdp"),
        P("fsdp"),
        P("fsdp"),
        P("fsdp"),
        P(None, "fsdp"),
        P("fsdp"),
        P("fsdp", None),
        P("fsdp"),
        P(None, "fsdp"),
        P("fsdp"),
    )
    return jax.shard_map(
        per_device, mesh=mesh, in_specs=in_specs, out_specs=out_specs, check_vma=False
    )
```

profile of v0, /device:TPU:0, one launch (start us, length us, event | category | flops | bytes accessed | tf_op | source)
XLA Modules:
  0.0 898.0 jit_solution(2339973718000685500)
XLA Ops:
  23.0 64.2 %all-reduce.21 = (bf16[768]{0:T(1024)(128)(2,1)S(1)}, bf16[768]{0:T(1024)(128)(2,1)S(1)}, bf16[768]{0:T(1024)(128)(2,1)S(1)}, bf16[768]{0:T(1024)(128)(2,1)S(1)}...) all-reduce(bf16[768]{0:T(1024)(128)(2,1)S(1)} %dynamic-update-slice, ...), channel_id=1, replica_groups=mesh['dp'=2,'fsdp'=16] {'fsdp'}, use_global_device_ids=true, to_apply=%add.1 | all-reduce | flops 10240 | bytes 40960
  94.5 7.4 convert_reduce_fusion.3
  121.2 70.8 %while.27 = (s32[]{:T(128)}, bf16[2,512,12,64]{1,3,2,0:T(8,128)(2,1)S(1)}, f32[2,12,512]{2,1,0:T(8,128)S(1)}, s32[2]{0:T(128)S(1)}, s32[1024]{0:T(1024)S(1)}, /*...) while((s32[]{:T(128)}, ...), condition=%wide.region_9.10_spmd, body=%wide.region_2.9_spmd.sunk | while | flops 1684282880 | bytes 95670480 | solution.py:92
  134.1 7.6 exponential_reduce_fusion.5
  169.3 7.6 exponential_reduce_fusion.5
  201.0 38.0 %multiply_convert_fusion.3 = (bf16[1024,3072]{1,0:T(8,128)(2,1)}, f32[1024,3072]{1,0:T(8,128)}, f32[1024,3072]{1,0:T(8,128)}) fusion(f32[3072]{0:T(1024)S(1)} %copy-done.56, bf16[768,3072]{0,1:T(8,128)(2,1)} %all-gather.10.cloned.1.call-done, f32[1024,768]{0,1:T(8,128)} %copy-done.13, f32[768]{0:T(1024)S(1)} %copy-done.60, f32[768]{0:T(1024)S(1)} %copy-done.50, ...), kind=kOutput, calls=%fused_computation.163 | convolution fusion | flops 5043388416 | bytes 39348224 | tf_op jit(solution)/shard_map/dot_general | solution.py:23
  239.0 9.1 %all-gather.12.cloned.1.call-done = bf16[3072,768]{1,0:T(8,128)(2,1)} async-done(((bf16[192,768]{1,0:T(8,128)(2,1)}), bf16[3072,768]{1,0:T(8,128)(2,1)}) %all-gather.12.cloned.1.call-update) | async-done | bytes 4718608 | tf_op jit(solution)/shard_map/all_gather | solution.py:205
  248.1 17.7 %convert_reduce_fusion = (f32[3072]{0:T(1024)}, bf16[1024,3072]{1,0:T(8,128)(2,1)}) fusion(f32[1024,3072]{1,0:T(8,128)} %get-tuple-element.412, bf16[1024,768]{0,1:T(8,128)(2,1)S(1)} %copy-done.70, bf16[3072,768]{1,0:T(8,128)(2,1)} %all-gather.12.cloned.1.call-done, f32[1024,3072]{1,0:T(8,128)} %get-tuple-element.433, f32[3072]{0:T(1024)S(1)} %copy-done.56), kind=kOutput, calls=%fused_computation.161 | convolution fusion | flops 4885312512 | bytes 37773312 | tf_op jit(solution)/shard_map/dot_general | solution.py:27
  265.8 10.3 %fusion.168 = (f32[768]{0:T(1024)}, f32[1024,768]{1,0:T(8,128)}) fusion(bf16[1024,3072]{1,0:T(8,128)(2,1)} %get-tuple-element.440, bf16[768,3072]{0,1:T(8,128)(2,1)} %all-gather.10.cloned.1.call-done), kind=kOutput, calls=%fused_computation.251 | convolution fusion | flops 4832623616 | bytes 14158848 | tf_op jit(solution)/shard_map/dot_general | solution.py:27
  306.5 9.0 %multiply_convert_fusion.4 = bf16[1024,768]{0,1:T(8,128)(2,1)S(1)} fusion(f32[1024,768]{0,1:T(8,128)S(1)} %copy-done.14, bf16[1024,3072]{1,0:T(8,128)(2,1)} %get-tuple-element.411, bf16[3072,768]{1,0:T(8,128)(2,1)} %all-gather.12.cloned.1.call-done, f32[768]{0:T(1024)S(1)} %convert_element_type.261, f32[1024]{0:T(1024)S(1)} %get-tuple-element.754), kind=kOutput, calls=%fused_computation.211 | convolution fusion | flops 4834983936 | bytes 15735808 | tf_op jit(solution)/shard_map/dot_general | solution.py:23
  321.7 185.8 %while.28 = (s32[]{:T(128)}, f32[1024,12,64]{0,2,1:T(8,128)}, f32[1024,12,64]{0,2,1:T(8,128)}, bf16[2,512,12,64]{1,3,2,0:T(8,128)(2,1)}, bf16[2,512,12,64]{1,3,2...) while((s32[]{:T(128)}, f32[1024,12,64]{0,2,1:T(8,128)}, ...), condition=%wide.region_18.19_spmd.clone, body=%wide.region_14.18_spmd.clone.sunk | while | flops 4133219840 | bytes 424604224 | solution.py:160
  356.1 21.4 %multiply_reduce_fusion.7 = (f32[4,512]{1,0:T(4,128)S(1)}, f32[4,512]{1,0:T(4,128)S(1)}, f32[4,512]{1,0:T(4,128)S(1)}, f32[4,512,1024]{2,1,0:T(8,128)}) fusion(f32[4,512,1024]{2,1,0:T(8,128)} %copy-done.2, f32[4,512]{1,0:T(4,128)S(1)} %get-tuple-element.613, pred[512,1024]{1,0:T(8,128)(4,1)S(1)} %fusion.301, f32[4,512,1024]{2,1,0:T(8,128)} %fusion.302, ...), kind=kOutput, calls=%fused_computation.64.clone.1 | convolution fusion | flops 299886592 | bytes 52215812 | tf_op jit(solution)/shard_map/while/body/eval_jaxpr/qhd,khd->hqk/dot_general | solution.py:119
  377.4 17.8 %multiply_convert_fusion.6 = (bf16[4,512,1024]{2,1,0:T(8,128)(2,1)S(1)}, bf16[4,512,1024]{2,1,0:T(8,128)(2,1)S(1)}, bf16[4,512,1024]{2,1,0:T(8,128)(2,1)S(1)}) fusion(f32[4,512,1024]{2,1,0:T(8,128)} %get-tuple-element.616, f32[4,512,1024]{2,1,0:T(8,128)} %copy-done.2, f32[4,512]{1,0:T(4,128)S(1)} %get-tuple-element.617, ...), kind=kLoop, calls=%fused_computation.63.clone.1 | loop fusion | flops 37748736 | bytes 63488000 | tf_op jit(solution)/shard_map/while/body/eval_jaxpr/convert_element_type | solution.py:126
  449.3 20.5 %multiply_reduce_fusion.7 = (f32[4,512]{1,0:T(4,128)S(1)}, f32[4,512]{1,0:T(4,128)S(1)}, f32[4,512]{1,0:T(4,128)S(1)}, f32[4,512,1024]{2,1,0:T(8,128)}) fusion(f32[4,512,1024]{2,1,0:T(8,128)} %copy-done.2, f32[4,512]{1,0:T(4,128)S(1)} %get-tuple-element.613, pred[512,1024]{1,0:T(8,128)(4,1)S(1)} %fusion.301, f32[4,512,1024]{2,1,0:T(8,128)} %fusion.302, ...), kind=kOutput, calls=%fused_computation.64.clone.1 | convolution fusion | flops 299886592 | bytes 52215812 | tf_op jit(solution)/shard_map/while/body/eval_jaxpr/qhd,khd->hqk/dot_general | solution.py:119
  469.8 17.4 %multiply_convert_fusion.6 = (bf16[4,512,1024]{2,1,0:T(8,128)(2,1)S(1)}, bf16[4,512,1024]{2,1,0:T(8,128)(2,1)S(1)}, bf16[4,512,1024]{2,1,0:T(8,128)(2,1)S(1)}) fusion(f32[4,512,1024]{2,1,0:T(8,128)} %get-tuple-element.616, f32[4,512,1024]{2,1,0:T(8,128)} %copy-done.2, f32[4,512]{1,0:T(4,128)S(1)} %get-tuple-element.617, ...), kind=kLoop, calls=%fused_computation.63.clone.1 | loop fusion | flops 37748736 | bytes 63488000 | tf_op jit(solution)/shard_map/while/body/eval_jaxpr/convert_element_type | solution.py:126
  514.5 6.9 fusion.148
  521.5 9.9 %fusion.170 = f32[3072,768]{1,0:T(8,128)} fusion(bf16[1024,3072]{1,0:T(8,128)(2,1)} %get-tuple-element.411, bf16[1024,768]{0,1:T(8,128)(2,1)} %get-tuple-element.404), kind=kOutput, calls=%fused_computation.253 | convolution fusion | flops 4831838208 | bytes 17301504 | tf_op jit(solution)/shard_map/dot_general | solution.py:33
  532.1 11.6 %fusion.159 = f32[768,3072]{0,1:T(8,128)} fusion(bf16[1024,3072]{1,0:T(8,128)(2,1)} %get-tuple-element.440, f32[1024,768]{0,1:T(8,128)} %copy-done.13, f32[768]{0:T(1024)S(1)} %copy-done.61, f32[768]{0:T(1024)S(1)} %copy-done.51, f32[1024]{0:T(1024)S(1)} %copy-done.53, f32[1024]{0:T(1024)S(1)} %copy-done.43), kind=kOutput, calls=%fused_computation.245 | convolution fusion | flops 4835770368 | bytes 18888704 | tf_op jit(solution)/shard_map/dot_general | solution.py:33
  550.8 9.3 %fusion.167 = (f32[768]{0:T(1024)S(1)}, f32[1024,768]{1,0:T(8,128)}) fusion(bf16[768,2304]{0,1:T(8,128)(2,1)} %all-gather.6.cloned.1.call-done, bf16[1024,768]{0,1:T(8,128)(2,1)} %bitcast.231, bf16[1024,768]{0,1:T(8,128)(2,1)} %bitcast.229, bf16[1024,768]{0,1:T(8,128)(2,1)} %bitcast.225), kind=kOutput, calls=%fused_computation.250 | convolution fusion | flops 3638820096 | bytes 11406336 | tf_op jit(solution)/shard_map/dot_general | solution.py:27
  567.9 60.8 %all-reduce.20 = (bf16[768]{0:T(1024)(128)(2,1)S(1)}, bf16[768]{0:T(1024)(128)(2,1)S(1)}, bf16[768]{0:T(1024)(128)(2,1)S(1)}, bf16[768]{0:T(1024)(128)(2,1)S(1)}...) all-reduce(f32[768]{0:T(1024)S(1)} %reduce_sum.261, ...), channel_id=3, replica_groups=mesh['dp'=2,'fsdp'=16] {'fsdp'}, use_global_device_ids=true, to_apply=%region_24.25.clone | all-reduce | flops 10240 | bytes 61440
  644.6 80.6 %reduce-scatter.12.cloned.1.call-done = f32[192,768]{1,0:T(8,128)} async-done(((f32[3072,768]{1,0:T(8,128)}), f32[192,768]{1,0:T(8,128)}) %reduce-scatter.12.cloned.1.call-update) | async-done | bytes 589840 | tf_op jit(solution)/shard_map/reduce_scatter | solution.py:342
  727.0 113.0 %reduce-scatter.10.cloned.1.call-done = f32[768,192]{0,1:T(8,128)} async-done(((f32[768,3072]{0,1:T(8,128)}), f32[768,192]{0,1:T(8,128)}) %reduce-scatter.10.cloned.1.call-update) | async-done | bytes 589840 | tf_op jit(solution)/shard_map/reduce_scatter | solution.py:340
  841.9 6.6 add_convert_fusion.2
  854.6 28.1 %all-reduce.26.cloned.1.call-done = (bf16[768,144]{0,1:T(8,128)(2,1)}, bf16[48,768]{1,0:T(8,128)(2,1)}, bf16[768,192]{0,1:T(8,128)(2,1)}, bf16[192,768]{1,0:T(8,128)(2,1)}, bf16[768,64]{0,1:T(8,128)(2,1)}) async-done(((bf16[768,144]{0,1:T(8,128)(2,1)}, bf16[48,768]{1,0:T(8,128)(2,1)}, bf16[768,192]{0,1:T(8,128)(2,1)}, bf16[192,768]{1,0:T(8,128)(2,1)}, bf16[768,64]{0,1:T(8,128)(2,1)}), ...) | async-done | bytes 983056 | tf_op jit(solution)/shard_map/psum | solution.py:348
  (384 shorter events, 294.8 us)
Async XLA Ops:
  7.2 87.3 %all-gather.14.cloned.1.call-start = ((), (), s32[]{:S(2)}) async-start(), calls=%async_computation.9 | async-start | bytes 1671168 | tf_op jit(solution)/shard_map/all_gather | solution.py:207
  7.9 94.0 %all-gather.6.cloned.1.call-start = ((), (), s32[]{:S(2)}) async-start(), calls=%async_computation.5 | async-start | bytes 3760128 | tf_op jit(solution)/shard_map/all_gather | solution.py:194
  8.7 186.7 %all-gather.8.cloned.1.call-start = ((), (), s32[]{:S(2)}) async-start(), calls=%async_computation.6 | async-start | bytes 1253376 | tf_op jit(solution)/shard_map/all_gather | solution.py:197
  9.4 191.6 %all-gather.10.cloned.1.call-start = ((), (), s32[]{:S(2)}) async-start(), calls=%async_computation.7 | async-start | bytes 5013504 | tf_op jit(solution)/shard_map/all_gather | solution.py:203
  10.0 238.2 %all-gather.12.cloned.1.call-start = ((), (), s32[]{:S(2)}) async-start(), calls=%async_computation.8 | async-start | bytes 5013504 | tf_op jit(solution)/shard_map/all_gather | solution.py:205
  10.6 629.2 %reduce-scatter.8.cloned.1.call-start = ((), (), s32[]{:S(2)}) async-start(), calls=%async_computation.11 | async-start | bytes 2506752 | tf_op jit(solution)/shard_map/reduce_scatter | solution.py:334
  87.3 14.6 %copy-start.62 = (f32[768]{0:T(1024)}, f32[768]{0:T(1024)S(1)}, u32[]{:S(2)}) copy-start(f32[768]{0:T(1024)S(1)} %convert_element_type.247) | copy-start | bytes 9220
  87.3 14.6 %copy-start.40 = (f32[768]{0:T(1024)}, f32[768]{0:T(1024)S(1)}, u32[]{:S(2)}) copy-start(f32[768]{0:T(1024)S(1)} %convert_element_type.246) | copy-start | bytes 9220
  91.4 10.5 %copy-start.8 = (bf16[1024,768]{0,1:T(8,128)(2,1)}, bf16[1024,768]{0,1:T(8,128)(2,1)S(1)}, u32[]{:S(2)}) copy-start(bf16[1024,768]{0,1:T(8,128)(2,1)S(1)} %copy.74) | copy-start | bytes 4718596
  91.7 10.3 %copy-start.38 = (f32[1024]{0:T(1024)}, f32[1024]{0:T(1024)S(1)}, u32[]{:S(2)}) copy-start(f32[1024]{0:T(1024)S(1)} %broadcast_multiply_fusion.1) | copy-start | bytes 12292
  92.7 9.2 %copy-start.46 = (f32[1024]{0:T(1024)}, f32[1024]{0:T(1024)S(1)}, u32[]{:S(2)}) copy-start(f32[1024]{0:T(1024)S(1)} %fusion.152) | copy-start | bytes 12292
  94.5 7.4 copy-start.20
  198.9 84.3 %copy-start.42 = (f32[1024]{0:T(1024)}, f32[1024]{0:T(1024)S(1)}, u32[]{:S(2)}) copy-start(f32[1024]{0:T(1024)S(1)} %broadcast_multiply_fusion) | copy-start | bytes 12292
  200.9 82.3 %copy-start.52 = (f32[1024]{0:T(1024)}, f32[1024]{0:T(1024)S(1)}, u32[]{:S(2)}) copy-start(f32[1024]{0:T(1024)S(1)} %fusion.153) | copy-start | bytes 12292
  200.9 47.2 %copy-start.70 = (bf16[1024,768]{0,1:T(8,128)(2,1)S(1)}, bf16[1024,768]{0,1:T(8,128)(2,1)}, u32[]{:S(2)}) copy-start(bf16[1024,768]{0,1:T(8,128)(2,1)} %get-tuple-element.404) | copy-start | bytes 4718596
  292.2 349.1 %reduce-scatter.14.cloned.1.call-start = ((), (), s32[]{:S(2)}) async-start(), calls=%async_computation.14 | async-start | bytes 3342336 | tf_op jit(solution)/shard_map/reduce_scatter | solution.py:344
  306.5 10.2 %copy-start.26 = (bf16[1024,1024]{1,0:T(8,128)(2,1)S(1)}, bf16[1024,1024]{1,0:T(8,128)(2,1)}, u32[]{:S(2)}) copy-start(bf16[1024,1024]{1,0:T(8,128)(2,1)} %param.43) | copy-start | bytes 6291460
  320.3 322.6 %reduce-scatter.6.cloned.1.call-start = ((), (), s32[]{:S(2)}) async-start(), calls=%async_computation.10 | async-start | bytes 7520256 | tf_op jit(solution)/shard_map/reduce_scatter | solution.py:331
  340.6 4.4 copy-start.2
  521.5 203.7 %reduce-scatter.12.cloned.1.call-start = ((), (), s32[]{:S(2)}) async-start(), calls=%async_computation.13 | async-start | bytes 10027008 | tf_op jit(solution)/shard_map/reduce_scatter | solution.py:342
  531.5 308.5 %reduce-scatter.10.cloned.1.call-start = ((), (), s32[]{:S(2)}) async-start(), calls=%async_computation.12 | async-start | bytes 10027008 | tf_op jit(solution)/shard_map/reduce_scatter | solution.py:340
  543.8 338.9 %all-reduce.26.cloned.1.call-start = ((), (), s32[]{:S(2)}) async-start(), calls=%async_computation.15 | async-start | bytes 1966080 | tf_op jit(solution)/shard_map/psum | solution.py:348
  567.8 274.0 %copy-start.22 = (bf16[1024,768]{0,1:T(8,128)(2,1)S(1)}, bf16[1024,768]{0,1:T(8,128)(2,1)}, u32[]{:S(2)}) copy-start(bf16[1024,768]{0,1:T(8,128)(2,1)} %copy-done.20) | copy-start | bytes 4718596
  567.8 274.1 %copy-start.45 = (f32[1024]{0:T(1024)S(1)}, f32[1024]{0:T(1024)}, u32[]{:S(2)}) copy-start(f32[1024]{0:T(1024)} %copy-done.44) | copy-start | bytes 12292
  (69 other events, 160.1 us)
Sparse Core Ops, SparseCore 0:
  10.3 42.2 all-gather.13
  54.9 45.9 all-gather.5
  103.2 36.9 all-gather.7
  142.3 51.9 all-gather.9
  196.4 51.6 all-gather.11
  292.3 61.7 reduce-scatter.7
  357.9 65.3 reduce-scatter.13
  521.6 88.7 reduce-scatter.5
  614.5 110.6 reduce-scatter.11
  729.1 110.8 reduce-scatter.9
  844.3 38.3 all-reduce.25
where the time goes:
time: 903 us; the launch traced here: 898 us
  matrix products  323 us (36%)
  waiting for transfers between devices  234 us (26%)
  blocking collectives  130 us (14%)
  other arithmetic  103 us (11%)
  local copies, waits for them, and re-layouts  78.6 us (9%)
  between operations  18.8 us (2%)
  loops' own time  9.5 us (1%)
    unnamed x2, blocking collectives  125 us
    reduce_scatter x1, waiting for transfers between devices, per_device(): lax.psum_scatter(grad_terms[9], 'fsdp', scatter_dimension=1, tiled=True)  113 us
    reduce_scatter x1, waiting for transfers between devices, per_device(): lax.psum_scatter(grad_terms[11], 'fsdp', scatter_dimension=0, tiled=True)  80.6 us
    dot_general x6, matrix products, one_block(): jnp.einsum('qhd,khd->hqk', grad_block[:, head_slice], value3[:, head_slic...  63.9 us
    dot_general x5, matrix products, product(): return jnp.dot(left, right, preferred_element_type=jnp.float32)  59.9 us
    dot_general x5, matrix products, product_right_t(): lax.dot_general(left, right, (((1,), (1,)), ((), ())), preferred_element_...  49 us
    dot_general x12, matrix products, masked_scores(): jnp.einsum('qhd,khd->hqk', query_part, key_part, preferred_element_type=j...  47.6 us
    convert_element_type x2, other arithmetic, one_block(): grad_scores = (attn_probs * (grad_probs - row_dot)).astype(jnp.bfloat16)  35.2 us
  transfers between devices with their start and end apart: 11, of which 4 were waited for; matrix products, arithmetic and copies ran while one was open for 48% of the time, Pallas kernels for 0%

commit v1 on v0

v1 whole, which is shorter than its diff:
```python
import functools

import jax
import jax.numpy as jnp
from jax import lax
from jax.experimental import pallas as pl
from jax.experimental.pallas import tpu as pltpu
from jax.sharding import PartitionSpec as P

HEADS = 12
F32 = jnp.float32
BF16 = jnp.bfloat16
NEG = -1e30


def nn(a, b):
    return lax.dot_general(a, b, (((1,), (0,)), ((), ())), preferred_element_type=F32)


def nt(a, b):
    return lax.dot_general(a, b, (((1,), (1,)), ((), ())), preferred_element_type=F32)


def tn(a, b):
    return lax.dot_general(a, b, (((0,), (0,)), ((), ())), preferred_element_type=F32)


def col_sum(v):
    return jnp.sum(v, 0, keepdims=True)


def gelu_parts(u):
    z = jnp.abs(u) * (0.5 ** 0.5)
    ez = jnp.exp(-(z * z))
    t = 1.0 / (1.0 + 0.33 * z)
    poly = -0.13593485572044933
    for coef in (0.46271278142719047, -0.3554798541586114, 0.412577688277986, 0.044992638979585504,
                 0.2019288303128453, 0.18283654298343202, 0.18636614548593147):
        poly = poly * t + coef
    half_erfc = (0.5 * t) * poly * ez
    cdf = jnp.where(u > 0, 1.0 - half_erfc, half_erfc)
    return u * cdf, cdf + u * ez * 0.3989422804014327


def row_stats(x):
    mean = jnp.mean(x, -1, keepdims=True)
    centered = x - mean
    rstd = lax.rsqrt(jnp.mean(centered * centered, -1, keepdims=True) + 1e-05)
    return centered * rstd, rstd


def norm_back(grad_hat, hat, rstd):
    return rstd * (grad_hat - jnp.mean(grad_hat, -1, keepdims=True)
                   - hat * jnp.mean(grad_hat * hat, -1, keepdims=True))


def call(kernel, grid, ins, outs, scratch=(), name=None, prefetch=(), limit=60):
    return pl.pallas_call(
        kernel,
        grid_spec=pltpu.PrefetchScalarGridSpec(
            num_scalar_prefetch=len(prefetch), grid=grid,
            in_specs=[pl.BlockSpec(b, m, **({"pipeline_mode": pl.Buffered(1)} if once else {}))
                      for _, b, m, once in ins],
            out_specs=[pl.BlockSpec(b, m) for _, _, b, m in outs],
            scratch_shapes=list(scratch)),
        out_shape=[jax.ShapeDtypeStruct(s, d) for s, d, _, _ in outs],
        compiler_params=pltpu.CompilerParams(
            dimension_semantics=("arbitrary",) * len(grid), vmem_limit_bytes=limit << 20),
        name=name,
    )(*prefetch, *[a for a, _, _, _ in ins])


def whole(a):
    n = a.ndim
    return (a, a.shape, lambda *_: (0,) * n, True)


def rows(a, tile):
    return (a, (tile, a.shape[1]), lambda i, *_: (i, 0), False)


def rows_out(n, width, dtype, tile):
    return ((n, width), dtype, (tile, width), lambda i, *_: (i, 0))


def fixed_out(shape, dtype):
    n = len(shape)
    return (shape, dtype, shape, lambda *_: (0,) * n)


def project(tokens, vecs, qkv_bias, qkv_t, tile=256):
    n, d = tokens.shape

    def kernel(x_ref, v_ref, b_ref, w_ref, n_ref, o_ref):
        hat, _ = row_stats(x_ref[...].astype(F32))
        low = (hat * v_ref[4:5, :] + v_ref[5:6, :]).astype(BF16)
        n_ref[...] = low
        for part in range(3):
            cols = pl.ds(part * d, d)
            o_ref[:, cols] = (nt(low, w_ref[cols, :]) + b_ref[:, cols]).astype(BF16)

    return call(
        kernel, (n // tile,),
        [rows(tokens, tile), whole(vecs), whole(qkv_bias), whole(qkv_t)],
        [rows_out(n, d, BF16, tile), rows_out(n, 3 * d, BF16, tile)],
        name="project")


def pair_masks(shape):
    lane = lax.broadcasted_iota(jnp.int32, shape, 1)
    return lane < 64


def attend(qkv, seg_col, key_row, ranges, tq=128, tk=256):
    n = qkv.shape[0]
    d = qkv.shape[1] // 3
    pairs = d // 128

    def kernel(rng, q_ref, k_ref, v_ref, sc_ref, kr_ref, o_ref, lse_ref, mask, sa, sb, va, vb):
        @pl.when(pl.program_id(0) == 0)
        def _():
            @pl.loop(0, n // tq)
            def _(t):
                r = pl.ds(pl.multiple_of(t * tq, tq), tq)
                row_id = t * tq + lax.broadcasted_iota(jnp.int32, (tq, n), 0)
                col_id = lax.broadcasted_iota(jnp.int32, (tq, n), 1)
                keep = (sc_ref[r, :] == kr_ref[...]) | (row_id == col_id)
                m = jnp.where(keep, 0.0, NEG).astype(F32)
                for j in range(n // tk):
                    mask[j, r, :] = m[:, j * tk:(j + 1) * tk]

        v = v_ref[...]
        low_half = pair_masks((n, 128))
        zero = jnp.zeros_like(v)
        va[...] = jnp.where(low_half, v, zero)
        vb[...] = jnp.where(low_half, zero, v)
        half = pair_masks((tq, 128))

        @pl.loop(0, n // tq)
        def _(t):
            r = pl.ds(pl.multiple_of(t * tq, tq), tq)
            q = q_ref[r, :] * jnp.asarray(0.125, BF16)
            qz = jnp.zeros_like(q)
            qa = jnp.where(half, q, qz)
            qb = jnp.where(half, qz, q)
            lo, hi = rng[0, t], rng[1, t]

            def score(j, carry):
                ma, mb = carry
                kk = k_ref[pl.ds(pl.multiple_of(j * tk, tk), tk), :]
                m = mask[j, r, :]
                s = nt(qa, kk) + m
                sa[j] = s
                for e in range(0, tk, 128):
                    ma = jnp.maximum(ma, s[:, e:e + 128])
                s = nt(qb, kk) + m
                sb[j] = s
                for e in range(0, tk, 128):
                    mb = jnp.maximum(mb, s[:, e:e + 128])
                return ma, mb

            start = jnp.full((tq, 128), NEG, F32)
            ma, mb = lax.fori_loop(lo, hi, score, (start, start))
            ma = jnp.max(ma, 1, keepdims=True)
            mb = jnp.max(mb, 1, keepdims=True)

            def mix(j, carry):
                la, lb, acc = carry
                keys = pl.ds(pl.multiple_of(j * tk, tk), tk)
                p = jnp.exp(sa[j] - ma)
                for e in range(0, tk, 128):
                    la = la + p[:, e:e + 128]
                a1 = nn(p.astype(BF16), va[keys, :])
                p = jnp.exp(sb[j] - mb)
                for e in range(0, tk, 128):
                    lb = lb + p[:, e:e + 128]
                return la, lb, acc + a1 + nn(p.astype(BF16), vb[keys, :])

            nil = jnp.zeros((tq, 128), F32)
            la, lb, acc = lax.fori_loop(lo, hi, mix, (nil, nil, nil))
            la = jnp.sum(la, 1, keepdims=True)
            lb = jnp.sum(lb, 1, keepdims=True)
            o_ref[r, :] = (acc * jnp.where(half, 1.0 / la, 1.0 / lb)).astype(BF16)
            lse = jnp.where(half, ma + jnp.log(la), mb + jnp.log(lb)).T
            lse_ref[0:1, r] = lse[0:1, :]
            lse_ref[1:2, r] = lse[64:65, :]

    def block(first):
        return (qkv, (n, 128), lambda p, *_: (0, first * pairs + p), False)

    return call(
        kernel, (pairs,),
        [block(0), block(1), block(2), whole(seg_col), whole(key_row)],
        [((n, d), BF16, (n, 128), lambda p, *_: (0, p)),
         ((8 * pairs, n), F32, (8, n), lambda p, *_: (p, 0))],
        [pltpu.VMEM((n // tk, n, tk), F32), pltpu.VMEM((n // tk, tq, tk), F32),
         pltpu.VMEM((n // tk, tq, tk), F32), pltpu.VMEM((n, 128), BF16), pltpu.VMEM((n, 128), BF16)],
        name="attend", prefetch=(ranges,))


def attend_back(qkv, mixed, grad_mixed, lse, seg_row, key_col, ranges, tk=256, tq=256):
    n = qkv.shape[0]
    d = qkv.shape[1] // 3
    pairs = d // 128

    def kernel(rng, q_ref, k_ref, v_ref, o_ref, g_ref, lse_ref, sr_ref, kc_ref,
               dq_ref, dk_ref, dv_ref, bq_ref, bv_ref, mask, qa, qb, ga, gb, kt, dot_rows, dqt):
        @pl.when(pl.program_id(0) == 0)
        def _():
            @pl.loop(0, n // tk)
            def _(t):
                r = pl.ds(pl.multiple_of(t * tk, tk), tk)
                row_id = t * tk + lax.broadcasted_iota(jnp.int32, (tk, n), 0)
                col_id = lax.broadcasted_iota(jnp.int32, (tk, n), 1)
                keep = (kc_ref[r, :] == sr_ref[...]) | (row_id == col_id)
                m = jnp.where(keep, 0.0, NEG).astype(F32)
                for j in range(n // tq):
                    mask[j, r, :] = m[:, j * tq:(j + 1) * tq]

        half = pair_masks((n, 128))
        q = q_ref[...] * jnp.asarray(0.125, BF16)
        zero = jnp.zeros_like(q)
        qa[...] = jnp.where(half, q, zero)
        qb[...] = jnp.where(half, zero, q)
        g = g_ref[...]
        ga[...] = jnp.where(half, g, zero)
        gb[...] = jnp.where(half, zero, g)
        kt[...] = k_ref[...].astype(F32).T.astype(BF16)
        prod = (g.astype(F32) * o_ref[...].astype(F32)).T
        dot_rows[0:1, :] = col_sum(prod[:64])
        dot_rows[1:2, :] = col_sum(prod[64:])
        dqt[...] = jnp.zeros_like(dqt)

        @pl.loop(0, n // tk)
        def _(t):
            keys = pl.ds(pl.multiple_of(t * tk, tk), tk)
            kk = k_ref[keys, :]
            vv = v_ref[keys, :]

            def step(j, carry):
                dk, dv = carry
                cols = pl.ds(pl.multiple_of(j * tq, tq), tq)
                m = mask[j, keys, :]
                for h, (qh, gh) in enumerate(((qa, ga), (qb, gb))):
                    qq = qh[cols, :]
                    gg = gh[cols, :]
                    p = jnp.exp(nt(kk, qq) + m - lse_ref[h:h + 1, cols])
                    ds = (p * (nt(vv, gg) - dot_rows[h:h + 1, cols])).astype(BF16)
                    dv = dv + nn(p.astype(BF16), gg)
                    dk = dk + nn(ds, qq)
                    part = pl.ds(64 * h, 64)
                    dqt[part, cols] += nn(kt[part, keys], ds)
                return dk, dv

            nil = jnp.zeros((tk, 128), F32)
            dk, dv = lax.fori_loop(rng[0, t], rng[1, t], step, (nil, nil))
            dk_ref[keys, :] = dk.astype(BF16)
            dv_ref[keys, :] = dv.astype(BF16)

        dq = (dqt[...].T * 0.125).astype(BF16)
        dq_ref[...] = dq
        bq_ref[...] = jnp.broadcast_to(col_sum(dq.astype(F32)), (8, 128))
        bv_ref[...] = jnp.broadcast_to(col_sum(dv_ref[...].astype(F32)), (8, 128))

    def block(a, first=0):
        return (a, (n, 128), lambda p, *_: (0, first * pairs + p), False)

    cols = ((n, d), BF16, (n, 128), lambda p, *_: (0, p))
    sums = ((8, d), F32, (8, 128), lambda p, *_: (0, p))
    return call(
        kernel, (pairs,),
        [block(qkv, 0), block(qkv, 1), block(qkv, 2), block(mixed), block(grad_mixed),
         (lse, (8, n), lambda p, *_: (p, 0), False), whole(seg_row), whole(key_col)],
        [cols, cols, cols, sums, sums],
        [pltpu.VMEM((n // tq, n, tq), F32)] + [pltpu.VMEM((n, 128), BF16)] * 4
        + [pltpu.VMEM((128, n), BF16), pltpu.VMEM((8, n), F32), pltpu.VMEM((128, n), F32)],
        name="attend_back", prefetch=(ranges,))


def middle(tokens, mixed, grad_output, grad_aligned, valid_col, vecs, up_b, align_b,
           out_w, up_t, down_w, align_t, tile=256, chunk=768):
    n, d = tokens.shape
    ff, al = up_t.shape[0], align_t.shape[0]

    def kernel(x_ref, m_ref, go_ref, ga_ref, v_ref, vec_ref, ub_ref, ab_ref, wo_ref, wu_ref, wd_ref, wa_ref,
               n_ref, act_ref, du_ref, gb_ref, out_ref, al_ref, r_ref, rb_ref, dm_ref,
               s768_ref, sff_ref, sal_ref, branch, dn):
        @pl.when(pl.program_id(0) == 0)
        def _():
            s768_ref[...] = jnp.zeros_like(s768_ref)
            sff_ref[...] = jnp.zeros_like(sff_ref)
            sal_ref[...] = jnp.zeros_like(sal_ref)

        resid = x_ref[...].astype(F32) + nn(m_ref[...], wo_ref[...]) + vec_ref[2:3, :]
        hat, rstd = row_stats(resid)
        low = (hat * vec_ref[6:7, :] + vec_ref[7:8, :]).astype(BF16)
        n_ref[...] = low
        valid = v_ref[...]
        ga = ga_ref[...]
        sal_ref[0:1, :] += col_sum(ga.astype(F32))
        grad = valid * (go_ref[...].astype(F32) + nn(ga, wa_ref[...]))
        gb = grad.astype(BF16)
        gb_ref[...] = gb
        branch[...] = jnp.zeros_like(branch)
        dn[...] = jnp.zeros_like(dn)

        @pl.loop(0, ff // chunk)
        def _(t):
            part = pl.ds(pl.multiple_of(t * chunk, chunk), chunk)
            wu = wu_ref[part, :]
            wd = wd_ref[part, :]
            act, slope = gelu_parts(nt(n_ref[...], wu) + ub_ref[0:1, part])
            act = act.astype(BF16)
            act_ref[:, part] = act
            branch[...] += nn(act, wd)
            du = slope * nt(gb_ref[...], wd)
            du = du.astype(BF16)
            du_ref[:, part] = du
            sff_ref[0:1, part] += col_sum(du.astype(F32))
            dn[...] += nn(du, wu)

        out = (valid * (resid + branch[...] + vec_ref[3:4, :])).astype(BF16)
        out_ref[...] = out
        al_ref[...] = (nt(out, wa_ref[...]) + ab_ref[...]).astype(BF16)
        dn2 = dn[...]
        res = grad + norm_back(dn2 * vec_ref[6:7, :], hat, rstd)
        r_ref[...] = res
        rb = res.astype(BF16)
        rb_ref[...] = rb
        dm_ref[...] = nt(rb, wo_ref[...]).astype(BF16)
        s768_ref[0:1, :] += col_sum(gb.astype(F32))
        s768_ref[1:2, :] += col_sum(rb.astype(F32))
        s768_ref[2:3, :] += col_sum(dn2 * hat)
        s768_ref[3:4, :] += col_sum(dn2)

    r = functools.partial(rows_out, n, tile=tile)
    return call(
        kernel, (n // tile,),
        [rows(tokens, tile), rows(mixed, tile), rows(grad_output, tile), rows(grad_aligned, tile),
         rows(valid_col, tile), whole(vecs), whole(up_b), whole(align_b), whole(out_w), whole(up_t),
         whole(down_w), whole(align_t)],
        [r(d, BF16), r(ff, BF16), r(ff, BF16), r(d, BF16), r(d, BF16), r(al, BF16), r(d, F32), r(d, BF16),
         r(d, BF16), fixed_out((8, d), F32), fixed_out((8, ff), F32), fixed_out((8, al), F32)],
        [pltpu.VMEM((tile, d), F32), pltpu.VMEM((tile, d), F32)],
        name="middle")


def finish(tokens, resid_grad, dq, dk, dv, vecs, qkv_t, tile=256):
    n, d = tokens.shape

    def kernel(x_ref, r_ref, dq_ref, dk_ref, dv_ref, vec_ref, w_ref, o_ref, s_ref):
        @pl.when(pl.program_id(0) == 0)
        def _():
            s_ref[...] = jnp.zeros_like(s_ref)

        dn = nn(dq_ref[...], w_ref[0:d, :]) + nn(dk_ref[...], w_ref[d:2 * d, :]) + nn(dv_ref[...], w_ref[2 * d:, :])
        hat, rstd = row_stats(x_ref[...].astype(F32))
        o_ref[...] = (r_ref[...] + norm_back(dn * vec_ref[4:5, :], hat, rstd)).astype(BF16)
        s_ref[0:1, :] += col_sum(dn * hat)
        s_ref[1:2, :] += col_sum(dn)

    return call(
        kernel, (n // tile,),
        [rows(tokens, tile), rows(resid_grad, tile), rows(dq, tile), rows(dk, tile), rows(dv, tile),
         whole(vecs), whole(qkv_t)],
        [rows_out(n, d, BF16, tile), fixed_out((8, d), F32)],
        name="finish")
MESHID = pl.DeviceIdType.MESH


def coords():
    y = lax.axis_index("dp")
    f = lax.axis_index("fsdp")
    return y, f // 4, lax.rem(f // 2, 2), lax.rem(f, 2)


def fs(z, x, c):
    return z * 4 + x * 2 + c


def gather_body(items, nz, ins, outs, ssem, rsem, lsem):
    y, z, x, c = coords()
    me = fs(z, x, c)

    def dev(yy, zz, xx, cc):
        return (yy, fs(zz, xx, cc))

    zp = [lax.rem(z + d, nz) for d in range(nz)]
    zm = [lax.rem(z - d + nz, nz) for d in range(nz)]
    sib = dev(y, z, x, 1 - c)
    xn = dev(y, z, 1 - x, c)
    yn = dev(1 - y, z, x, c)

    barrier = pltpu.get_barrier_semaphore()
    peers = [sib, xn, yn] + [dev(y, zp[d], x, c) for d in range(1, nz)]
    for p in peers:
        pl.semaphore_signal(barrier, inc=1, device_id=p, device_id_type=MESHID)
    pl.semaphore_wait(barrier, len(peers))

    started = []
    NS = 6 * nz + 8

    class It:
        pass

    def rowspan(i, kind):
        a, r0, rows, third = items[i]
        if kind == "all":
            return r0, rows
        if kind == "plane":
            return r0 + y * third, rows - third
        if kind == "mine":
            return r0 + y * (rows - third), third
        if kind == "theirs":
            return r0 + (1 - y) * (rows - third), third

    def full(i, shard, kind):
        a = items[i][0]
        rw = ins[a].shape[0]
        r0, n = rowspan(i, kind)
        return outs[a].at[pl.ds(pl.multiple_of(shard * rw + r0, 8), n)]

    def own(i, kind):
        a = items[i][0]
        r0, n = rowspan(i, kind)
        return ins[a].at[pl.ds(pl.multiple_of(r0, 8), n)]

    COL, OTH, YY, SIB = 0, nz, 2 * nz, 4 * nz

    def copy(i, src, dst, slot, to):
        n = len([1 for s in started if s[0] == i])
        cp = pltpu.make_async_remote_copy(
            src_ref=src, dst_ref=dst, send_sem=ssem.at[i, n], recv_sem=rsem.at[i, slot],
            device_id=to, device_id_type=MESHID)
        cp.start()
        started.append((i, cp))

    def wait_in(i, shard, kind, slot):
        ref = full(i, shard, kind)
        pltpu.make_async_remote_copy(
            src_ref=ref, dst_ref=ref, send_sem=ssem.at[i, 0], recv_sem=rsem.at[i, slot],
            device_id=sib, device_id_type=MESHID).wait_recv()

    locals_ = []

    def start_own(i):
        cp = pltpu.make_async_copy(own(i, "all"), full(i, me, "all"), lsem.at[i])
        cp.start()
        locals_.append(cp)
        for d in range(1, nz):
            copy(i, own(i, "plane"), full(i, me, "plane"), COL + d, dev(y, zp[d], x, c))
        copy(i, own(i, "plane"), full(i, me, "plane"), OTH + 0, xn)
        copy(i, own(i, "all"), full(i, me, "all"), SIB + 0, sib)

    def stage_col(i):
        for d in range(1, nz):
            sh = fs(zm[d], x, c)
            wait_in(i, sh, "plane", COL + d)
            copy(i, full(i, sh, "plane"), full(i, sh, "plane"), OTH + d, xn)
            copy(i, full(i, sh, "mine"), full(i, sh, "mine"), YY + d, yn)
            copy(i, full(i, sh, "plane"), full(i, sh, "plane"), SIB + d, sib)

    def stage_oth(i):
        for d in range(nz):
            sh = fs(zm[d], 1 - x, c)
            wait_in(i, sh, "plane", OTH + d)
            copy(i, full(i, sh, "mine"), full(i, sh, "mine"), YY + nz + d, yn)
            copy(i, full(i, sh, "plane"), full(i, sh, "plane"), SIB + nz + d, sib)

    def stage_y(i):
        for d in range(1, 2 * nz):
            sh = fs(zm[d % nz], x if d < nz else 1 - x, c)
            wait_in(i, sh, "theirs", YY + d)
            copy(i, full(i, sh, "theirs"), full(i, sh, "theirs"), SIB + 2 * nz + d, sib)

    def stage_sib(i):
        wait_in(i, fs(z, x, 1 - c), "all", SIB + 0)
        for d in range(1, 2 * nz):
            sh = fs(zm[d % nz], x if d < nz else 1 - x, 1 - c)
            wait_in(i, sh, "plane", SIB + d)
            wait_in(i, sh, "theirs", SIB + 2 * nz + d)

    n = len(items)
    for i in range(n):
        start_own(i)
    for t in range(n + 3):
        if t < n:
            stage_col(t)
        if 0 <= t - 1 < n:
            stage_oth(t - 1)
        if 0 <= t - 2 < n:
            stage_y(t - 2)
        if 0 <= t - 3 < n:
            stage_sib(t - 3)
    for cp in locals_:
        cp.wait()
    for _, cp in started:
        cp.wait_send()


def gather_call(items, shards, nz, cid=0):
    n_in = len(shards)

    def kern(*refs):
        ins, outs = refs[:n_in], refs[n_in:2 * n_in]
        ssem, rsem, lsem = refs[2 * n_in:]
        gather_body(items, nz, ins, outs, ssem, rsem, lsem)

    n_items = len(items)
    return pl.pallas_call(
        kern,
        out_shape=[jax.ShapeDtypeStruct((4 * nz * s.shape[0], s.shape[1]), s.dtype) for s in shards],
        in_specs=[pl.BlockSpec(memory_space=pltpu.VMEM)] * n_in,
        out_specs=[pl.BlockSpec(memory_space=pl.ANY)] * n_in,
        scratch_shapes=[
            pltpu.SemaphoreType.DMA((n_items, 8 * nz)),
            pltpu.SemaphoreType.DMA((n_items, 8 * nz)),
            pltpu.SemaphoreType.DMA((n_items,)),
        ],
        compiler_params=pltpu.CompilerParams(collective_id=cid, has_side_effects=True),
        name="gather_weights",
    )(*shards)


def third_of(n):
    return max(16, n // 3 // 16 * 16)


def gather_all(shards, fast):
    if not fast:
        return [lax.all_gather(s, "fsdp", axis=0, tiled=True) for s in shards]
    *big, pack = shards
    nz = 4
    order = [(5, 0, pack.shape[0], 8 if pack.shape[0] >= 24 else 0)]
    return gather_call(GATHER_ITEMS(shards), shards, nz)


def GATHER_ITEMS(shards):
    items = []
    for i in (5, 0, 1, 2, 3, 4):
        r = shards[i].shape[0]
        items.append((i, 0, r, third_of(r)))
    return items
def weight_grads_reduced(pairs, pack, shard_rows, cuts, blocks, nz, collective):
    nw = len(pairs)
    lefts = [a for ls, _ in pairs for a in ls]
    rights = [r for _, r in pairs]
    n = rights[0].shape[0]
    width = rights[0].shape[1]
    max_left = max(sum(a.shape[1] for a in ls) for ls, _ in pairs)
    items = [(w, j) for w in range(nw) for j in range(width // blocks[w])]
    ni = len(items)

    def kernel(*refs):
        left_refs = refs[:len(lefts)]
        right_refs = refs[len(lefts):len(lefts) + nw]
        pos = len(lefts) + nw
        pack_ref = refs[pos]
        out_refs = refs[pos + 1:pos + 1 + nw]
        pack_out = refs[pos + 1 + nw]
        pos += 2 + nw
        lbuf, rbuf = refs[pos:pos + 2]
        part, sibb, yb, xb, zb, fin, finb = [refs[pos + 2 + k * nw:pos + 2 + (k + 1) * nw] for k in range(7)]
        pos += 2 + 7 * nw
        pbuf, ssem, rsem, psem, prsem, lsem = refs[pos:]

        y, z, x, c = coords()

        def dev(yy, zz, xx, cc):
            return (yy, zz * 4 + xx * 2 + cc)

        sib, xn, yn = dev(y, z, x, 1 - c), dev(y, z, 1 - x, c), dev(1 - y, z, x, c)
        zp = [lax.rem(z + d, nz) for d in range(nz)]
        zd = [dev(y, zp[d], x, c) for d in range(nz)]

        barrier = pltpu.get_barrier_semaphore()
        peers = [sib, xn, yn] + zd[1:]
        for p in peers:
            pl.semaphore_signal(barrier, inc=1, device_id=p, device_id_type=MESHID)

        loads = {}

        def load(w):
            at = 0
            got = []
            first = sum(len(ls) for ls, _ in pairs[:w])
            for k in range(len(pairs[w][0])):
                ref = left_refs[first + k]
                cols = ref.shape[1]
                cp = pltpu.make_async_copy(ref, lbuf.at[w % 2, :, pl.ds(at, cols)], lsem.at[w, k])
                cp.start()
                got.append(cp)
                at += cols
            cp = pltpu.make_async_copy(right_refs[w], rbuf.at[w % 2], lsem.at[w, 3])
            cp.start()
            got.append(cp)
            loads[w] = got

        started = []

        def send(i, k, src, dst, to):
            cp = pltpu.make_async_remote_copy(
                src_ref=src, dst_ref=dst, send_sem=ssem.at[i, k], recv_sem=rsem.at[i, k],
                device_id=to, device_id_type=MESHID)
            cp.start()
            started.append(cp)
            return cp

        flight = {}

        def spans(w):
            rw, a = shard_rows[w], cuts[w]
            return dict(plane=(y * a, rw - a), mine=(y * (rw - a), a), theirs=((1 - y) * (rw - a), a))

        def rows_of(w, kind):
            r0, k = spans(w)[kind]
            return pl.ds(pl.multiple_of(r0, 16), k)

        def compute(i):
            w, j = items[i]
            rw, lb = shard_rows[w], blocks[w]
            if j == 0:
                for cp in loads[w]:
                    cp.wait()
            cols = pl.ds(j * lb, lb)
            right = rbuf[w % 2, :, cols]
            for half in range(nz // 2):
                left = lbuf[w % 2, :, pl.ds(half * 8 * rw, 8 * rw)]
                g = tn(left, right).astype(BF16)
                for k in range(8):
                    part[w][j, k % 2, (k // 2) % 2, 2 * half + k // 4] = g[k * rw:(k + 1) * rw]
            if j == width // lb - 1 and w + 2 < nw:
                load(w + 2)
            flight[i, 0] = send(i, 0, part[w].at[j, 1 - c], sibb[w].at[j], sib)

        def stage_sib(i):
            w, j = items[i]
            flight[i, 0].wait_recv()
            mine = part[w].at[j, c]
            for xx in range(2):
                for zz in range(nz):
                    mine[xx, zz] = (mine[xx, zz].astype(F32) + sibb[w][j, xx, zz].astype(F32)).astype(BF16)
            flight[i, 1] = send(i, 1, mine.at[:, :, rows_of(w, "theirs")], yb[w].at[j], yn)

        def stage_y(i):
            w, j = items[i]
            flight[i, 1].wait_recv()
            mine = part[w].at[j, c]
            r = rows_of(w, "mine")
            for xx in range(2):
                for zz in range(nz):
                    mine[xx, zz, r] = (mine[xx, zz, r].astype(F32) + yb[w][j, xx, zz].astype(F32)).astype(BF16)
            flight[i, 2] = send(i, 2, mine.at[1 - x, :, rows_of(w, "plane")], xb[w].at[j], xn)

        def stage_x(i):
            w, j = items[i]
            flight[i, 2].wait_recv()
            mine = part[w].at[j, c, x]
            r = rows_of(w, "plane")
            for zz in range(nz):
                mine[zz, r] = (mine[zz, r].astype(F32) + xb[w][j, zz].astype(F32)).astype(BF16)
            for d in range(1, nz):
                flight[i, 2 + d] = send(i, 2 + d, mine.at[zp[d], r], zb[w].at[j, d - 1], zd[d])

        def stage_z(i):
            w, j = items[i]
            total = part[w][j, c, x, z, rows_of(w, "plane")].astype(F32)
            for d in range(1, nz):
                flight[i, 2 + d].wait_recv()
                total = total + zb[w][j, d - 1].astype(F32)
            fin[w][j] = total.astype(BF16)
            flight[i, 2 + nz] = send(i, 2 + nz, fin[w].at[j], finb[w].at[j], yn)

        def stage_out(i):
            w, j = items[i]
            rw, a, lb = shard_rows[w], cuts[w], blocks[w]
            cols = pl.ds(j * lb, lb)
            flight[i, 2 + nz].wait_recv()
            here, there = fin[w].at[j], finb[w].at[j]

            def at(r0, k):
                return pl.ds(pl.multiple_of(r0, 16), k)

            out_refs[w][at(y * (rw - a), a), cols] = here[at(y * (rw - 2 * a), a)].astype(F32)
            out_refs[w][at((1 - y) * (rw - a), a), cols] = there[at((1 - y) * (rw - 2 * a), a)].astype(F32)
            if rw > 2 * a:
                out_refs[w][pl.ds(a, rw - 2 * a), cols] = (
                    here[at((1 - y) * a, rw - 2 * a)].astype(F32) + there[at(y * a, rw - 2 * a)].astype(F32))

        pack_to = [sib, yn, xn, dev(y, z + 1 - 2 * lax.rem(z, 2), x, c), dev(y, lax.rem(z + 2, 4), x, c)]
        pack_cp = {}

        def pack_step(k):
            if k > 0:
                pack_cp[k - 1].wait()
                pbuf[0, k] = pbuf[0, k - 1] + pbuf[1, k - 1]
            else:
                pbuf[0, 0] = pack_ref[...]
            if k < len(pack_to):
                cp = pltpu.make_async_remote_copy(
                    src_ref=pbuf.at[0, k], dst_ref=pbuf.at[1, k], send_sem=psem.at[k], recv_sem=prsem.at[k],
                    device_id=pack_to[k], device_id_type=MESHID)
                cp.start()
                pack_cp[k] = cp
            else:
                pack_out[...] = pbuf[0, k]

        load(0)
        load(1)
        pl.semaphore_wait(barrier, len(peers))
        stages = [compute, stage_sib, stage_y, stage_x, stage_z, stage_out]
        for t in range(ni + len(stages) - 1):
            for k, stage in enumerate(stages):
                if 0 <= t - k < ni:
                    stage(t - k)
            if t <= len(pack_to):
                pack_step(t)
        for cp in started:
            cp.wait_send()

    any_spec = pl.BlockSpec(memory_space=pl.ANY)
    vm = pl.BlockSpec(memory_space=pltpu.VMEM)

    def per_weight(make):
        return [pltpu.VMEM(make(width // b, shard_rows[w], cuts[w], b), BF16) for w, b in enumerate(blocks)]

    scratch = [pltpu.VMEM((2, n, max_left), BF16), pltpu.VMEM((2, n, width), BF16)]
    scratch += per_weight(lambda j, rw, a, b: (j, 2, 2, nz, rw, b))
    scratch += per_weight(lambda j, rw, a, b: (j, 2, nz, rw, b))
    scratch += per_weight(lambda j, rw, a, b: (j, 2, nz, a, b))
    scratch += per_weight(lambda j, rw, a, b: (j, nz, rw - a, b))
    scratch += per_weight(lambda j, rw, a, b: (j, nz - 1, rw - a, b))
    scratch += per_weight(lambda j, rw, a, b: (j, rw - a, b))
    scratch += per_weight(lambda j, rw, a, b: (j, rw - a, b))
    scratch += [
        pltpu.VMEM((2, 6) + pack.shape, F32),
        pltpu.SemaphoreType.DMA((ni, 3 + nz)), pltpu.SemaphoreType.DMA((ni, 3 + nz)),
        pltpu.SemaphoreType.DMA((6,)), pltpu.SemaphoreType.DMA((6,)), pltpu.SemaphoreType.DMA((nw, 4)),
    ]
    outs = pl.pallas_call(
        kernel,
        out_shape=[jax.ShapeDtypeStruct((rw, width), F32) for rw in shard_rows]
        + [jax.ShapeDtypeStruct(pack.shape, F32)],
        in_specs=[any_spec] * (len(lefts) + nw) + [vm],
        out_specs=[vm] * (nw + 1),
        scratch_shapes=scratch,
        compiler_params=pltpu.CompilerParams(
            collective_id=collective, has_side_effects=True, vmem_limit_bytes=63 << 20),
        name="reduce_grads",
    )(*lefts, *rights, pack)
    return outs[:nw], outs[nw]


def reduce_all(pairs, pack, fast):
    if fast:
        left_rows = [sum(a.shape[1] for a in ls) for ls, _ in pairs]
        shard_rows = [r // 16 for r in left_rows]
        cuts = [max(16, (r * 5 // 16) // 16 * 16) for r in shard_rows]
        blocks = [384, 256, 256, 768, 256]
        return weight_grads_reduced(pairs, pack, shard_rows, cuts, blocks, 4, 1)
    terms = [jnp.concatenate([tn(a, r).astype(BF16) for a in ls], 0) for ls, r in pairs]
    got = [lax.psum(lax.psum_scatter(t, "fsdp", scatter_dimension=0, tiled=True), "dp").astype(F32) for t in terms]
    return got, lax.psum(pack, ("dp", "fsdp"))
def per_device(mesh_shape, *args):
    (tokens, segment_ids, padding, qkv_weight, query_bias, value_bias, out_weight, out_bias,
     first_gain, first_shift, second_gain, second_shift, up_weight, up_bias, down_weight, down_bias,
     align_weight, align_bias, grad_output, grad_aligned) = args
    n, d = tokens.shape
    shards = [qkv_weight.T, out_weight, up_weight.T, down_weight, align_weight.T]
    small = [query_bias, value_bias, out_bias, down_bias, first_gain, first_shift, second_gain, second_shift]
    fast = mesh_shape["dp"] == 2 and mesh_shape["fsdp"] == 16
    own = query_bias.shape[0]
    pack = jnp.concatenate(small + [up_bias, align_bias])
    pad = -pack.shape[0] % (48 * 128)
    pack = jnp.pad(pack, (0, pad)).reshape(-1, 128)
    gathered = gather_all(shards + [pack], fast)
    qkv_t, out_w, up_t, down_w, align_t, packs = gathered
    members = mesh_shape["fsdp"]
    packs = packs.reshape(members, -1).astype(F32)
    vecs = packs[:, :8 * own].reshape(members, 8, own).transpose(1, 0, 2).reshape(8, d)
    ub, ab = up_bias.shape[0], align_bias.shape[0]
    up_b = packs[:, 8 * own:8 * own + ub].reshape(1, -1)
    align_b = packs[:, 8 * own + ub:8 * own + ub + ab].reshape(1, -1)
    qkv_b = jnp.concatenate([vecs[0:1], jnp.zeros((1, d), F32), vecs[1:2]], 1)

    seg = segment_ids[0]
    pad_row = padding[0]
    keys = jnp.where(pad_row == 0, seg, -1)
    valid_col = (1.0 - pad_row.astype(F32))[:, None]

    def ranges(tile, block):
        first = seg[::tile]
        last = seg[tile - 1::tile]
        lo = jnp.sum(seg[None, :] < first[:, None], 1, dtype=jnp.int32) // block
        hi = (jnp.sum(seg[None, :] <= last[:, None], 1, dtype=jnp.int32) + block - 1) // block
        return jnp.stack([lo, hi])

    normed, qkv = project(tokens, vecs, qkv_b, qkv_t)
    mixed, lse = attend(qkv, seg[:, None], keys[None, :], ranges(128, 256))
    (n2, act, du, gb, block_out, aligned, res, rb, dm, s768, sff, sal) = middle(
        tokens, mixed, grad_output, grad_aligned, valid_col, vecs, up_b, align_b, out_w, up_t, down_w, align_t)
    dq, dk, dv, bq, bv = attend_back(qkv, mixed, dm, lse, seg[None, :], keys[:, None], ranges(256, 256))
    grad_tokens, s1 = finish(tokens, res, dq, dk, dv, vecs, qkv_t)

    sums = jnp.concatenate(
        [bq[0:1], bv[0:1], s768[1:2], s768[0:1], s1[0:2], s768[2:4]], 0)
    pack = jnp.concatenate([sums.reshape(-1), sff[0], sal[0]]).reshape(-1, 128)
    pairs = [([grad_aligned], block_out), ([act], gb), ([du], n2), ([mixed], rb), ([dq, dk, dv], normed)]
    (g_align, g_down, g_up, g_out, g_qkv), pack = reduce_all(pairs, pack, fast)
    me = lax.axis_index("fsdp")
    pack = pack.reshape(-1)
    vec = lax.dynamic_slice(pack[:8 * d].reshape(8, d), (0, me * own), (8, own))
    ff, al = up_t.shape[0], align_t.shape[0]
    g_ub = lax.dynamic_slice(pack, (8 * d + me * ub,), (ub,))
    g_ab = lax.dynamic_slice(pack, (8 * d + ff + me * ab,), (ab,))
    return (block_out, aligned, grad_tokens, g_qkv.T, vec[0], vec[1], g_out, vec[2], vec[4], vec[5], vec[6],
            vec[7], g_up.T, g_ub, g_down, vec[3], g_align.T, g_ab)


def solution(mesh):
    rows_spec = P(("dp", "fsdp"), None)
    vec, by_col, by_row = P("fsdp"), P(None, "fsdp"), P("fsdp", None)
    in_specs = (rows_spec, rows_spec, rows_spec, by_col, vec, vec, by_row, vec, vec, vec, vec, vec,
                by_col, vec, by_row, vec, by_col, vec, rows_spec, rows_spec)
    out_specs = (rows_spec, rows_spec, rows_spec, by_col, vec, vec, by_row, vec, vec, vec, vec, vec,
                 by_col, vec, by_row, vec, by_col, vec)
    return jax.shard_map(functools.partial(per_device, dict(mesh.shape)), mesh=mesh, in_specs=in_specs,
                         out_specs=out_specs, check_vma=False)
```

time: 903 us -> 414 us (0.46)
  Pallas kernels: 0 us -> 378 us
  matrix products: 323 us -> 0 us
  waiting for transfers between devices: 234 us -> 0 us
  blocking collectives: 130 us -> 0 us
  other arithmetic: 103 us -> 5 us
  local copies, waits for them, and re-layouts: 78.6 us -> 28.6 us
  between operations: 18.8 us -> 0.84 us
  loops' own time: 9.5 us -> 0 us
    pallas_call x0 -> x7, Pallas kernels: none -> 378 us  [the longest x5 193 us: call(): pl.pallas_call(kernel, grid_spec=pltpu.PrefetchScalarGridSpec(num_scalar_...]
    dot_general x57 -> x0, matrix products: 323 us -> none  [the longest x6 63.9 us: one_block(): jnp.einsum('qhd,khd->hqk', grad_block[:, head_slice], value3[:, head_slic...]
    reduce_scatter x5 -> x0, waiting for transfers between devices: 194 us -> none  [the longest x1 113 us: per_device(): lax.psum_scatter(grad_terms[9], 'fsdp', scatter_dimension=1, tiled=True)]
    unnamed x2 -> x0, blocking collectives: 125 us -> none
    convert_element_type x35 -> x0, other arithmetic: 70.9 us -> none  [the longest x2 35.2 us: one_block(): grad_scores = (attn_probs * (grad_probs - row_dot)).astype(jnp.bfloat16)]
    unnamed x158 -> x19, local copies, waits for them, and re-layouts: 34.9 us -> 5.76 us
    psum x1 -> x0, waiting for transfers between devices: 28.1 us -> none  [per_device(): lax.psum(owned[0].astype(jnp.bfloat16), 'dp').astype(jnp.float32)]
    reduce_sum x13 -> x2, other arithmetic: 22 us -> 1.13 us  [ranges(): lo = jnp.sum(seg[None, :] < first[:, None], 1, dtype=jnp.int32) // block]
  transfers between devices with their start and end apart: 11 -> 0, of which waited for: 4 -> 0; matrix products, arithmetic and copies ran while one was open for 48% -> 0% of each run, Pallas kernels for 0% -> 0%
where the time goes in v1:
time: 414 us; the launch traced here: 413 us
  Pallas kernels  378 us (91%)
  local copies, waits for them, and re-layouts  28.6 us (7%)
  other arithmetic  5 us (1%)
    pallas_call x5, Pallas kernels, call(): pl.pallas_call(kernel, grid_spec=pltpu.PrefetchScalarGridSpec(num_scalar_...  193 us
    pallas_call x1, Pallas kernels, weight_grads_reduced(): pl.pallas_call(kernel, out_shape=[jax.ShapeDtypeStruct((rw, width), F32)...  96.7 us
    pallas_call x1, Pallas kernels, gather_call(): pl.pallas_call(kern, out_shape=[jax.ShapeDtypeStruct((4 * nz * s.shape[0]...  88.9 us

profile of v1, /device:TPU:0, one launch (start us, length us, event | category | flops | bytes accessed | tf_op | source)
XLA Modules:
  0.0 412.7 jit_solution(5401933081552280743)
XLA Ops:
  0.7 0.8 slice.85
  1.4 0.8 slice.86
  2.2 0.9 convert_reduce_fusion.1
  3.7 6.8 %concatenate.12 = bf16[640]{0:T(1024)(128)(2,1)S(1)} concatenate(bf16[48]{0:T(256)(128)(2,1)} %param.24, bf16[48]{0:T(256)(128)(2,1)} %param.25, bf16[48]{0:T(256)(128)(2,1)} %param.27, bf16[48]{0:T(256)(128)(2,1)} %param.35, bf16[48]{0:T(256)(128)(2,1)} %param.28, bf16[48]{0:T(256)(128)(2,1)} %param.29, bf16[48]{0:T(256)(128)(2,1)} %param.30, bf16[48]{0:T(256)(128)(2,1)} %param.31, ...), dimensions={0} | concatenate | bytes 2560 | tf_op jit(solution)/shard_map/concatenate | solution.py:773
  11.1 88.9 %gather_weights.1 = (bf16[2304,768]{1,0:T(8,128)(2,1)}, bf16[768,768]{1,0:T(8,128)(2,1)}, bf16[3072,768]{1,0:T(8,128)(2,1)}, bf16[3072,768]{1,0:T(8,128)(2,1)}, ...) custom-call(bf16[144,768]{1,0:T(8,128)(2,1)} %bitcast.73, bf16[48,768]{1,0:T(8,128)(2,1)} %refs_1_.1, ...), custom_call_target="tpu_custom_call" | custom-call | tf_op jit(solution)/shard_map/gather_weights/pallas_call | solution.py:510
  99.9 1.0 reshape.327
  102.6 8.8 %project.1 = (bf16[1024,768]{1,0:T(8,128)(2,1)}, bf16[1024,2304]{1,0:T(8,128)(2,1)}) custom-call(bf16[1024,768]{1,0:T(8,128)(2,1)} %x_ref.5, f32[8,768]{1,0:T(8,128)} %reshape.320.v_ref.vec_ref, f32[1,2304]{1,0:T(1,128)} %fusion.b_ref, bf16[2304,768]{1,0:T(8,128)(2,1)} %get-tuple-element.54.w_ref), custom_call_target="tpu_custom_call" | custom-call | tf_op jit(solution)/shard_map/project/pallas_call | solution.py:58
  111.4 1.0 copy.44.sc_ref
  113.0 65.8 %attend.1 = (bf16[1024,768]{1,0:T(8,128)(2,1)}, f32[48,1024]{1,0:T(8,128)}) custom-call(s32[2,8]{1,0:T(2,128)} %pad_add_fusion.rng, bf16[1024,2304]{1,0:T(8,128)(2,1)} %get-tuple-element.55.q_ref.k_ref.v_ref, bf16[1024,2304]{1,0:T(8,128)(2,1)} %get-tuple-element.55.q_ref.k_ref.v_ref, bf16[1024,2304]{1,0:T(8,128)(2,1)} %get-tuple-element.55.q_ref.k_ref.v_ref, ...), custom_call_target="tpu_custom_call" | custom-call | tf_op jit(solution)/shard_map/attend/pallas_call | solution.py:58
  180.2 1.0 copy.45.v_ref
  181.3 52.6 %middle.1 = (bf16[1024,768]{1,0:T(8,128)(2,1)}, bf16[1024,3072]{1,0:T(8,128)(2,1)}, bf16[1024,3072]{1,0:T(8,128)(2,1)}, bf16[1024,768]{1,0:T(8,128)(2,1)}, bf16[...) custom-call(bf16[1024,768]{1,0:T(8,128)(2,1)} %x_ref.5, ...), custom_call_target="tpu_custom_call" | custom-call | tf_op jit(solution)/shard_map/middle/pallas_call | solution.py:58
  235.2 0.8 broadcast_select_fusion.kc_ref
  236.0 55.7 %attend_back.1 = (bf16[1024,768]{1,0:T(8,128)(2,1)}, bf16[1024,768]{1,0:T(8,128)(2,1)}, bf16[1024,768]{1,0:T(8,128)(2,1)}, f32[8,768]{1,0:T(8,128)}, f32[8,768]{1,0:T(8,128)}) custom-call(s32[2,4]{1,0:T(2,128)} %pad_add_fusion.1.rng, bf16[1024,2304]{1,0:T(8,128)(2,1)} %get-tuple-element.55.q_ref.k_ref.v_ref, ...), custom_call_target="tpu_custom_call" | custom-call | tf_op jit(solution)/shard_map/attend_back/pallas_call | solution.py:58
  291.7 9.9 %finish.1 = (bf16[1024,768]{1,0:T(8,128)(2,1)}, f32[8,768]{1,0:T(8,128)}) custom-call(bf16[1024,768]{1,0:T(8,128)(2,1)} %x_ref.5, f32[1024,768]{1,0:T(8,128)} %get-tuple-element.63.r_ref, bf16[1024,768]{1,0:T(8,128)(2,1)} %get-tuple-element.66.dq_ref.refs_4_, bf16[1024,768]{1,0:T(8,128)(2,1)} %get-tuple-element.67.dk_ref.refs_5_, ...), custom_call_target="tpu_custom_call" | custom-call | tf_op jit(solution)/shard_map/finish/pallas_call | solution.py:58
  303.9 0.9 slice.102
  304.8 0.8 slice.103
  306.2 96.7 %reduce_grads.1 = (f32[64,768]{1,0:T(8,128)}, f32[192,768]{1,0:T(8,128)}, f32[192,768]{1,0:T(8,128)}, f32[48,768]{1,0:T(8,128)}, f32[144,768]{1,0:T(8,128)}, /*index=5*/f32[80,128]{1,0:T(8,128)}) custom-call(bf16[1024,1024]{1,0:T(8,128)(2,1)} %refs_0_.1, bf16[1024,3072]{1,0:T(8,128)(2,1)} %get-tuple-element.70.refs_1_, ...), custom_call_target="tpu_custom_call" | custom-call | tf_op jit(solution)/shard_map/reduce_grads/pallas_call | solution.py:740
  403.0 0.8 slice.104
  404.4 1.3 dynamic_slice.10
  405.7 1.3 dynamic_slice.11
  407.0 1.8 copy.53
  408.8 1.6 copy.54
  410.4 0.8 copy.55
  411.2 0.8 copy.56
  (52 shorter events, 10.3 us)
Async XLA Ops:
  102.6 8.8 %copy-start.4 = (s32[1,1024]{1,0:T(1,128)S(1)}, s32[1,1024]{1,0:T(1,128)}, u32[]{:S(2)}) copy-start(s32[1,1024]{1,0:T(1,128)} %sr_ref.1) | copy-start | bytes 12292
  102.6 9.8 %copy-start.5 = (s32[1,1024]{1,0:T(1,128)S(1)}, s32[1,1024]{1,0:T(1,128)}, u32[]{:S(2)}) copy-start(s32[1,1024]{1,0:T(1,128)} %param.22) | copy-start | bytes 12292
  181.3 53.9 %copy-start = (s32[1024,1]{1,0:T(8,128)S(1)}, s32[1024,1]{1,0:T(8,128)}, u32[]{:S(2)}) copy-start(s32[1024,1]{1,0:T(8,128)} %copy.44.sc_ref) | copy-start | bytes 12292
  291.7 12.1 %copy-start.6 = (f32[8,768]{1,0:T(8,128)S(1)}, f32[8,768]{1,0:T(8,128)}, u32[]{:S(2)}) copy-start(f32[8,768]{1,0:T(8,128)} %get-tuple-element.78) | copy-start | bytes 73732
  402.9 7.5 %copy-start.2 = (f32[192,768]{1,0:T(8,128)S(1)}, f32[192,768]{1,0:T(8,128)}, u32[]{:S(2)}) copy-start(f32[192,768]{1,0:T(8,128)} %get-tuple-element.85) | copy-start | bytes 1769476
  402.9 8.3 %copy-start.1 = (f32[192,768]{1,0:T(8,128)S(1)}, f32[192,768]{1,0:T(8,128)}, u32[]{:S(2)}) copy-start(f32[192,768]{1,0:T(8,128)} %get-tuple-element.140) | copy-start | bytes 1769476
  407.0 5.1 %copy-start.3 = (f32[64,768]{1,0:T(8,128)S(1)}, f32[64,768]{1,0:T(8,128)}, u32[]{:S(2)}) copy-start(f32[64,768]{1,0:T(8,128)} %get-tuple-element.87) | copy-start | bytes 589828

commit v2 on v1

--- a/solution.py
+++ b/solution.py
@@ -111,24 +111,35 @@
     return lane < 64
 
 
-def attend(qkv, seg_col, key_row, ranges, tq=128, tk=256):
+def windows(seg, tile, step=256):
+    n = seg.shape[0]
+    first = seg[::tile]
+    last = seg[tile - 1::tile]
+    lo = jnp.sum(seg[None, :] < first[:, None], 1, dtype=jnp.int32) // 128 * 128
+    hi = jnp.sum(seg[None, :] <= last[:, None], 1, dtype=jnp.int32)
+    count = (hi - lo + step - 1) // step
+    return jnp.stack([jnp.minimum(lo, n - count * step), count])
+
+
+def fill_mask(mask, rows_ref, cols_ref, n, tile=256):
+    @pl.when(pl.program_id(0) == 0)
+    def _():
+        @pl.loop(0, n // tile)
+        def _(t):
+            r = pl.ds(pl.multiple_of(t * tile, tile), tile)
+            row_id = t * tile + lax.broadcasted_iota(jnp.int32, (tile, n), 0)
+            col_id = lax.broadcasted_iota(jnp.int32, (tile, n), 1)
+            keep = (rows_ref[r, :] == cols_ref[...]) | (row_id == col_id)
+            mask[r, :] = jnp.where(keep, 0.0, NEG).astype(F32)
+
+
+def attend(qkv, seg_col, key_row, wins, tq=256, step=256):
     n = qkv.shape[0]
     d = qkv.shape[1] // 3
     pairs = d // 128
 
-    def kernel(rng, q_ref, k_ref, v_ref, sc_ref, kr_ref, o_ref, lse_ref, mask, sa, sb, va, vb):
-        @pl.when(pl.program_id(0) == 0)
-        def _():
-            @pl.loop(0, n // tq)
-            def _(t):
-                r = pl.ds(pl.multiple_of(t * tq, tq), tq)
-                row_id = t * tq + lax.broadcasted_iota(jnp.int32, (tq, n), 0)
-                col_id = lax.broadcasted_iota(jnp.int32, (tq, n), 1)
-                keep = (sc_ref[r, :] == kr_ref[...]) | (row_id == col_id)
-                m = jnp.where(keep, 0.0, NEG).astype(F32)
-                for j in range(n // tk):
-                    mask[j, r, :] = m[:, j * tk:(j + 1) * tk]
-
+    def kernel(win, q_ref, k_ref, v_ref, sc_ref, kr_ref, o_ref, lse_ref, mask, va, vb):
+        fill_mask(mask, sc_ref, kr_ref, n)
         v = v_ref[...]
         low_half = pair_masks((n, 128))
         zero = jnp.zeros_like(v)
@@ -139,51 +150,28 @@
         @pl.loop(0, n // tq)
         def _(t):
             r = pl.ds(pl.multiple_of(t * tq, tq), tq)
-            q = q_ref[r, :] * jnp.asarray(0.125, BF16)
-            qz = jnp.zeros_like(q)
-            qa = jnp.where(half, q, qz)
-            qb = jnp.where(half, qz, q)
-            lo, hi = rng[0, t], rng[1, t]
-
-            def score(j, carry):
-                ma, mb = carry
-                kk = k_ref[pl.ds(pl.multiple_of(j * tk, tk), tk), :]
-                m = mask[j, r, :]
-                s = nt(qa, kk) + m
-                sa[j] = s
-                for e in range(0, tk, 128):
-                    ma = jnp.maximum(ma, s[:, e:e + 128])
-                s = nt(qb, kk) + m
-                sb[j] = s
-                for e in range(0, tk, 128):
-                    mb = jnp.maximum(mb, s[:, e:e + 128])
-                return ma, mb
-
-            start = jnp.full((tq, 128), NEG, F32)
-            ma, mb = lax.fori_loop(lo, hi, score, (start, start))
-            ma = jnp.max(ma, 1, keepdims=True)
-            mb = jnp.max(mb, 1, keepdims=True)
-
-            def mix(j, carry):
-                la, lb, acc = carry
-                keys = pl.ds(pl.multiple_of(j * tk, tk), tk)
-                p = jnp.exp(sa[j] - ma)
-                for e in range(0, tk, 128):
-                    la = la + p[:, e:e + 128]
-                a1 = nn(p.astype(BF16), va[keys, :])
-                p = jnp.exp(sb[j] - mb)
-                for e in range(0, tk, 128):
-                    lb = lb + p[:, e:e + 128]
-                return la, lb, acc + a1 + nn(p.astype(BF16), vb[keys, :])
-
-            nil = jnp.zeros((tq, 128), F32)
-            la, lb, acc = lax.fori_loop(lo, hi, mix, (nil, nil, nil))
-            la = jnp.sum(la, 1, keepdims=True)
-            lb = jnp.sum(lb, 1, keepdims=True)
-            o_ref[r, :] = (acc * jnp.where(half, 1.0 / la, 1.0 / lb)).astype(BF16)
-            lse = jnp.where(half, ma + jnp.log(la), mb + jnp.log(lb)).T
-            lse_ref[0:1, r] = lse[0:1, :]
-            lse_ref[1:2, r] = lse[64:65, :]
+            first = pl.multiple_of(win[0, t], 128)
+
+            for count in range(1, n // step + 1):
+                @pl.when(win[1, t] == count)
+                def _():
+                    keys = pl.ds(first, count * step)
+                    q = q_ref[r, :] * jnp.asarray(0.125, BF16)
+                    qz = jnp.zeros_like(q)
+                    kk = k_ref[keys, :]
+                    outs, tops, sums = [], [], []
+                    for qh, vh in ((jnp.where(half, q, qz), va), (jnp.where(half, qz, q), vb)):
+                        s = nt(qh, kk) + mask[r, keys]
+                        top = jnp.max(s, 1, keepdims=True)
+                        p = jnp.exp(s - top)
+                        sums.append(jnp.sum(p, 1, keepdims=True))
+                        tops.append(top)
+                        outs.append(nn(p.astype(BF16), vh[keys, :]))
+                    (la, lb), (ma, mb) = sums, tops
+                    o_ref[r, :] = ((outs[0] + outs[1]) * jnp.where(half, 1.0 / la, 1.0 / lb)).astype(BF16)
+                    lse = jnp.where(half, ma + jnp.log(la), mb + jnp.log(lb)).T
+                    lse_ref[0:1, r] = lse[0:1, :]
+                    lse_ref[1:2, r] = lse[64:65, :]
 
     def block(first):
         return (qkv, (n, 128), lambda p, *_: (0, first * pairs + p), False)
@@ -193,30 +181,18 @@
         [block(0), block(1), block(2), whole(seg_col), whole(key_row)],
         [((n, d), BF16, (n, 128), lambda p, *_: (0, p)),
          ((8 * pairs, n), F32, (8, n), lambda p, *_: (p, 0))],
-        [pltpu.VMEM((n // tk, n, tk), F32), pltpu.VMEM((n // tk, tq, tk), F32),
-         pltpu.VMEM((n // tk, tq, tk), F32), pltpu.VMEM((n, 128), BF16), pltpu.VMEM((n, 128), BF16)],
-        name="attend", prefetch=(ranges,))
-
-
-def attend_back(qkv, mixed, grad_mixed, lse, seg_row, key_col, ranges, tk=256, tq=256):
+        [pltpu.VMEM((n, n), F32), pltpu.VMEM((n, 128), BF16), pltpu.VMEM((n, 128), BF16)],
+        name="attend", prefetch=(wins,))
+
+
+def attend_back(qkv, mixed, grad_mixed, lse, seg_row, key_col, wins, tk=256, step=256):
     n = qkv.shape[0]
     d = qkv.shape[1] // 3
     pairs = d // 128
 
-    def kernel(rng, q_ref, k_ref, v_ref, o_ref, g_ref, lse_ref, sr_ref, kc_ref,
-               dq_ref, dk_ref, dv_ref, bq_ref, bv_ref, mask, qa, qb, ga, gb, kt, dot_rows, dqt):
-        @pl.when(pl.program_id(0) == 0)
-        def _():
-            @pl.loop(0, n // tk)
-            def _(t):
-                r = pl.ds(pl.multiple_of(t * tk, tk), tk)
-                row_id = t * tk + lax.broadcasted_iota(jnp.int32, (tk, n), 0)
-                col_id = lax.broadcasted_iota(jnp.int32, (tk, n), 1)
-                keep = (kc_ref[r, :] == sr_ref[...]) | (row_id == col_id)
-                m = jnp.where(keep, 0.0, NEG).astype(F32)
-                for j in range(n // tq):
-                    mask[j, r, :] = m[:, j * tq:(j + 1) * tq]
-
+    def kernel(win, q_ref, k_ref, v_ref, o_ref, g_ref, lse_ref, sr_ref, kc_ref,
+               dq_ref, dk_ref, dv_ref, bq_ref, bv_ref, mask, qa, qb, ga, gb, kt, dots, dqt):
+        fill_mask(mask, kc_ref, sr_ref, n)
         half = pair_masks((n, 128))
         q = q_ref[...] * jnp.asarray(0.125, BF16)
         zero = jnp.zeros_like(q)
@@ -227,35 +203,37 @@
         gb[...] = jnp.where(half, zero, g)
         kt[...] = k_ref[...].astype(F32).T.astype(BF16)
         prod = (g.astype(F32) * o_ref[...].astype(F32)).T
-        dot_rows[0:1, :] = col_sum(prod[:64])
-        dot_rows[1:2, :] = col_sum(prod[64:])
+        dots[0:1, :] = col_sum(prod[:64])
+        dots[1:2, :] = col_sum(prod[64:])
         dqt[...] = jnp.zeros_like(dqt)
 
         @pl.loop(0, n // tk)
         def _(t):
             keys = pl.ds(pl.multiple_of(t * tk, tk), tk)
-            kk = k_ref[keys, :]
-            vv = v_ref[keys, :]
-
-            def step(j, carry):
-                dk, dv = carry
-                cols = pl.ds(pl.multiple_of(j * tq, tq), tq)
-                m = mask[j, keys, :]
-                for h, (qh, gh) in enumerate(((qa, ga), (qb, gb))):
-                    qq = qh[cols, :]
-                    gg = gh[cols, :]
-                    p = jnp.exp(nt(kk, qq) + m - lse_ref[h:h + 1, cols])
-                    ds = (p * (nt(vv, gg) - dot_rows[h:h + 1, cols])).astype(BF16)
-                    dv = dv + nn(p.astype(BF16), gg)
-                    dk = dk + nn(ds, qq)
-                    part = pl.ds(64 * h, 64)
-                    dqt[part, cols] += nn(kt[part, keys], ds)
-                return dk, dv
-
-            nil = jnp.zeros((tk, 128), F32)
-            dk, dv = lax.fori_loop(rng[0, t], rng[1, t], step, (nil, nil))
-            dk_ref[keys, :] = dk.astype(BF16)
-            dv_ref[keys, :] = dv.astype(BF16)
+            first = pl.multiple_of(win[0, t], 128)
+
+            for count in range(1, n // step + 1):
+                @pl.when(win[1, t] == count)
+                def _():
+                    kk = k_ref[keys, :]
+                    vv = v_ref[keys, :]
+                    dk = dv = None
+                    for e in range(count):
+                        cols = pl.ds(pl.multiple_of(first + e * step, 128), step)
+                        m = mask[keys, cols]
+                        for h, (qh, gh) in enumerate(((qa, ga), (qb, gb))):
+                            qq = qh[cols, :]
+                            gg = gh[cols, :]
+                            p = jnp.exp(nt(kk, qq) + m - lse_ref[h:h + 1, cols])
+                            ds = (p * (nt(vv, gg) - dots[h:h + 1, cols])).astype(BF16)
+                            pv = nn(p.astype(BF16), gg)
+                            pk = nn(ds, qq)
+                            dv = pv if dv is None else dv + pv
+                            dk = pk if dk is None else dk + pk
+                            part = pl.ds(64 * h, 64)
+                            dqt[part, cols] += nn(kt[part, keys], ds)
+                    dk_ref[keys, :] = dk.astype(BF16)
+                    dv_ref[keys, :] = dv.astype(BF16)
 
         dq = (dqt[...].T * 0.125).astype(BF16)
         dq_ref[...] = dq
@@ -272,13 +250,13 @@
         [block(qkv, 0), block(qkv, 1), block(qkv, 2), block(mixed), block(grad_mixed),
          (lse, (8, n), lambda p, *_: (p, 0), False), whole(seg_row), whole(key_col)],
         [cols, cols, cols, sums, sums],
-        [pltpu.VMEM((n // tq, n, tq), F32)] + [pltpu.VMEM((n, 128), BF16)] * 4
+        [pltpu.VMEM((n, n), F32)] + [pltpu.VMEM((n, 128), BF16)] * 4
         + [pltpu.VMEM((128, n), BF16), pltpu.VMEM((8, n), F32), pltpu.VMEM((128, n), F32)],
-        name="attend_back", prefetch=(ranges,))
+        name="attend_back", prefetch=(wins,))
 
 
 def middle(tokens, mixed, grad_output, grad_aligned, valid_col, vecs, up_b, align_b,
-           out_w, up_t, down_w, align_t, tile=256, chunk=768):
+           out_w, up_t, down_w, align_t, tile=512, chunk=768):
     n, d = tokens.shape
     ff, al = up_t.shape[0], align_t.shape[0]
 
@@ -374,173 +352,240 @@
     return y, f // 4, lax.rem(f // 2, 2), lax.rem(f, 2)
 
 
-def fs(z, x, c):
-    return z * 4 + x * 2 + c
-
-
-def gather_body(items, nz, ins, outs, ssem, rsem, lsem):
-    y, z, x, c = coords()
-    me = fs(z, x, c)
-
-    def dev(yy, zz, xx, cc):
-        return (yy, fs(zz, xx, cc))
-
-    zp = [lax.rem(z + d, nz) for d in range(nz)]
-    zm = [lax.rem(z - d + nz, nz) for d in range(nz)]
-    sib = dev(y, z, x, 1 - c)
-    xn = dev(y, z, 1 - x, c)
-    yn = dev(1 - y, z, x, c)
-
-    barrier = pltpu.get_barrier_semaphore()
-    peers = [sib, xn, yn] + [dev(y, zp[d], x, c) for d in range(1, nz)]
-    for p in peers:
-        pl.semaphore_signal(barrier, inc=1, device_id=p, device_id_type=MESHID)
-    pl.semaphore_wait(barrier, len(peers))
-
-    started = []
-    NS = 6 * nz + 8
-
-    class It:
-        pass
-
-    def rowspan(i, kind):
-        a, r0, rows, third = items[i]
-        if kind == "all":
-            return r0, rows
-        if kind == "plane":
-            return r0 + y * third, rows - third
-        if kind == "mine":
-            return r0 + y * (rows - third), third
-        if kind == "theirs":
-            return r0 + (1 - y) * (rows - third), third
-
-    def full(i, shard, kind):
-        a = items[i][0]
-        rw = ins[a].shape[0]
-        r0, n = rowspan(i, kind)
-        return outs[a].at[pl.ds(pl.multiple_of(shard * rw + r0, 8), n)]
-
-    def own(i, kind):
-        a = items[i][0]
-        r0, n = rowspan(i, kind)
-        return ins[a].at[pl.ds(pl.multiple_of(r0, 8), n)]
-
-    COL, OTH, YY, SIB = 0, nz, 2 * nz, 4 * nz
-
-    def copy(i, src, dst, slot, to):
-        n = len([1 for s in started if s[0] == i])
-        cp = pltpu.make_async_remote_copy(
-            src_ref=src, dst_ref=dst, send_sem=ssem.at[i, n], recv_sem=rsem.at[i, slot],
+def at_rows(first, count):
+    return pl.ds(pl.multiple_of(first, 16), count)
+
+
+class Gather:
+    def __init__(self, items, nz, ssem, rsem, lsem):
+        self.items, self.nz, self.ssem, self.rsem, self.lsem = items, nz, ssem, rsem, lsem
+        self.y, self.z, self.x, self.c = coords()
+
+    def device(self, y=None, z=None, x=None, c=None):
+        pick = [own if new is None else new for own, new in zip((self.y, self.z, self.x, self.c), (y, z, x, c))]
+        return (pick[0], pick[1] * 4 + pick[2] * 2 + pick[3])
+
+    def ahead(self, d):
+        return lax.rem(self.z + d, self.nz)
+
+    def enter(self):
+        barrier = pltpu.get_barrier_semaphore()
+        peers = [self.device(c=1 - self.c), self.device(x=1 - self.x), self.device(y=1 - self.y)]
+        peers += [self.device(z=self.ahead(d)) for d in range(1, self.nz)]
+        for peer in peers:
+            pl.semaphore_signal(barrier, inc=1, device_id=peer, device_id_type=MESHID)
+        pl.semaphore_wait(barrier, len(peers))
+
+    def span(self, i, which):
+        _, _, lo, n, third = self.items[i]
+        return {"all": (lo, n), "plane": (lo + self.y * third, n - third),
+                "mine": (lo + self.y * (n - third), third)}[which]
+
+    def local(self, i):
+        own, full = self.items[i][:2]
+        r = at_rows(*self.span(i, "plane"))
+        return pltpu.make_async_copy(own.at[r], full.at[self.z, self.x, self.c, r], self.lsem.at[i])
+
+    def copy(self, i, k):
+        own, full = self.items[i][:2]
+        every = pl.ds(0, self.nz)
+        if k == 0:
+            ref = full.at[every, self.x, self.c, at_rows(*self.span(i, "plane"))]
+            src, to = ref, self.device(x=1 - self.x)
+        elif k == 1:
+            ref = full.at[every, :, self.c, at_rows(*self.span(i, "mine"))]
+            src, to = ref, self.device(y=1 - self.y)
+        elif k == 2:
+            ref = full.at[every, :, self.c, at_rows(*self.span(i, "all"))]
+            src, to = ref, self.device(c=1 - self.c)
+        else:
+            r = at_rows(*self.span(i, "plane"))
+            src, ref, to = own.at[r], full.at[self.z, self.x, self.c, r], self.device(z=self.ahead(k - 2))
+        return pltpu.make_async_remote_copy(
+            src_ref=src, dst_ref=ref, send_sem=self.ssem.at[i, k], recv_sem=self.rsem.at[i, k],
             device_id=to, device_id_type=MESHID)
-        cp.start()
-        started.append((i, cp))
-
-    def wait_in(i, shard, kind, slot):
-        ref = full(i, shard, kind)
-        pltpu.make_async_remote_copy(
-            src_ref=ref, dst_ref=ref, send_sem=ssem.at[i, 0], recv_sem=rsem.at[i, slot],
-            device_id=sib, device_id_type=MESHID).wait_recv()
-
-    locals_ = []
-
-    def start_own(i):
-        cp = pltpu.make_async_copy(own(i, "all"), full(i, me, "all"), lsem.at[i])
-        cp.start()
-        locals_.append(cp)
-        for d in range(1, nz):
-            copy(i, own(i, "plane"), full(i, me, "plane"), COL + d, dev(y, zp[d], x, c))
-        copy(i, own(i, "plane"), full(i, me, "plane"), OTH + 0, xn)
-        copy(i, own(i, "all"), full(i, me, "all"), SIB + 0, sib)
-
-    def stage_col(i):
-        for d in range(1, nz):
-            sh = fs(zm[d], x, c)
-            wait_in(i, sh, "plane", COL + d)
-            copy(i, full(i, sh, "plane"), full(i, sh, "plane"), OTH + d, xn)
-            copy(i, full(i, sh, "mine"), full(i, sh, "mine"), YY + d, yn)
-            copy(i, full(i, sh, "plane"), full(i, sh, "plane"), SIB + d, sib)
-
-    def stage_oth(i):
-        for d in range(nz):
-            sh = fs(zm[d], 1 - x, c)
-            wait_in(i, sh, "plane", OTH + d)
-            copy(i, full(i, sh, "mine"), full(i, sh, "mine"), YY + nz + d, yn)
-            copy(i, full(i, sh, "plane"), full(i, sh, "plane"), SIB + nz + d, sib)
-
-    def stage_y(i):
-        for d in range(1, 2 * nz):
-            sh = fs(zm[d % nz], x if d < nz else 1 - x, c)
-            wait_in(i, sh, "theirs", YY + d)
-            copy(i, full(i, sh, "theirs"), full(i, sh, "theirs"), SIB + 2 * nz + d, sib)
-
-    def stage_sib(i):
-        wait_in(i, fs(z, x, 1 - c), "all", SIB + 0)
-        for d in range(1, 2 * nz):
-            sh = fs(zm[d % nz], x if d < nz else 1 - x, 1 - c)
-            wait_in(i, sh, "plane", SIB + d)
-            wait_in(i, sh, "theirs", SIB + 2 * nz + d)
-
-    n = len(items)
-    for i in range(n):
-        start_own(i)
-    for t in range(n + 3):
-        if t < n:
-            stage_col(t)
-        if 0 <= t - 1 < n:
-            stage_oth(t - 1)
-        if 0 <= t - 2 < n:
-            stage_y(t - 2)
-        if 0 <= t - 3 < n:
-            stage_sib(t - 3)
-    for cp in locals_:
-        cp.wait()
-    for _, cp in started:
-        cp.wait_send()
-
-
-def gather_call(items, shards, nz, cid=0):
-    n_in = len(shards)
-
-    def kern(*refs):
-        ins, outs = refs[:n_in], refs[n_in:2 * n_in]
-        ssem, rsem, lsem = refs[2 * n_in:]
-        gather_body(items, nz, ins, outs, ssem, rsem, lsem)
-
-    n_items = len(items)
-    return pl.pallas_call(
-        kern,
-        out_shape=[jax.ShapeDtypeStruct((4 * nz * s.shape[0], s.shape[1]), s.dtype) for s in shards],
-        in_specs=[pl.BlockSpec(memory_space=pltpu.VMEM)] * n_in,
-        out_specs=[pl.BlockSpec(memory_space=pl.ANY)] * n_in,
-        scratch_shapes=[
-            pltpu.SemaphoreType.DMA((n_items, 8 * nz)),
-            pltpu.SemaphoreType.DMA((n_items, 8 * nz)),
-            pltpu.SemaphoreType.DMA((n_items,)),
-        ],
-        compiler_params=pltpu.CompilerParams(collective_id=cid, has_side_effects=True),
-        name="gather_weights",
-    )(*shards)
-
-
-def third_of(n):
-    return max(16, n // 3 // 16 * 16)
-
-
-def gather_all(shards, fast):
-    if not fast:
-        return [lax.all_gather(s, "fsdp", axis=0, tiled=True) for s in shards]
-    *big, pack = shards
-    nz = 4
-    order = [(5, 0, pack.shape[0], 8 if pack.shape[0] >= 24 else 0)]
-    return gather_call(GATHER_ITEMS(shards), shards, nz)
-
-
-def GATHER_ITEMS(shards):
-    items = []
-    for i in (5, 0, 1, 2, 3, 4):
-        r = shards[i].shape[0]
-        items.append((i, 0, r, third_of(r)))
-    return items
+
+    def start(self, i):
+        self.local(i).start()
+        for d in range(1, self.nz):
+            self.copy(i, 2 + d).start()
+
+    def pass_z(self, i):
+        for d in range(1, self.nz):
+            self.copy(i, 2 + d).wait_recv()
+        self.local(i).wait()
+        self.copy(i, 0).start()
+
+    def pass_x(self, i):
+        self.copy(i, 0).wait_recv()
+        self.copy(i, 1).start()
+
+    def pass_y(self, i):
+        self.copy(i, 1).wait_recv()
+        self.copy(i, 2).start()
+
+    def ready(self, i):
+        self.copy(i, 2).wait_recv()
+
+    def leave(self):
+        for i in range(len(self.items)):
+            for k in range(2 + self.nz):
+                self.copy(i, k).wait_send()
+
+    def events(self, link, hop):
+        sizes = [full.shape[-1] * n for _, full, _, n, _ in self.items]
+        out = []
+        z = x = y = 0.0
+        for i, size in enumerate(sizes):
+            t = link * size / sum(sizes)
+            z += t
+            x = max(x, z + hop) + t
+            y = max(y, x + hop) + t
+            out += [(z + hop, self.pass_z, i), (x + hop, self.pass_x, i), (y + hop, self.pass_y, i),
+                    (y + 2 * hop + t / 4, self.ready, i)]
+        return sorted(out, key=lambda e: (e[0], e[2]))
+
+
+def gather_attend(tokens, pack, shards, seg_col, key_row, own, nz, tile=512, tq=256, link=62.0, hop=2.0,
+                  start=5.0, slots=(4.8, 1.45)):
+    n, d = tokens.shape
+    members = 4 * nz
+    pairs = d // 128
+    heights = [s.shape[0] for s in shards]
+    cuts = [(1 + w, lo, min(48, h - lo) if h != 64 else 64) for w, h in enumerate(heights)
+            for lo in range(0, h if h != 64 else 1, 48)]
+    cuts = [(0, 0, pack.shape[0])] + cuts
+    first_use = 1 + len([c for c in cuts if c[0] == 1])
+    ni = len(cuts)
+
+    def kernel(x_ref, sc_ref, kr_ref, p_ref, *refs):
+        owns = (p_ref,) + refs[:5]
+        n_ref, qkv_ref, vec_ref, o_ref, lse_ref = refs[5:10]
+        fulls = refs[10:16]
+        mask, va, vb, ssem, rsem, lsem = refs[16:]
+        packs_ref, w_ref = fulls[:2]
+        g = Gather([(owns[w], fulls[w], lo, k, max(16, k // 3 // 16 * 16)) for w, lo, k in cuts], nz, ssem, rsem, lsem)
+        g.enter()
+        for i in range(ni):
+            g.start(i)
+
+        @pl.loop(0, n // tq)
+        def _(t):
+            r = pl.ds(pl.multiple_of(t * tq, tq), tq)
+            row_id = t * tq + lax.broadcasted_iota(jnp.int32, (tq, n), 0)
+            col_id = lax.broadcasted_iota(jnp.int32, (tq, n), 1)
+            keep = (sc_ref[r, :] == kr_ref[...]) | (row_id == col_id)
+            mask[r, :] = jnp.where(keep, 0.0, NEG).astype(F32)
+
+        events = g.events(link, hop)
+        now = start + max(t for t, f, i in events if i < first_use and f == g.ready)
+
+        def pump(until):
+            while events and start + events[0][0] <= until:
+                _, f, i = events.pop(0)
+                f(i)
+
+        pump(now)
+        plan = []
+        for k in range(n // tile + pairs * (n // tq)):
+            now += slots[0] if k < n // tile else slots[1]
+            mark = len([e for e in events if start + e[0] <= now])
+            plan.append(events[:mark])
+            del events[:mark]
+        total = jnp.zeros((16, d), F32)
+        row = lax.broadcasted_iota(jnp.int32, (128, d), 0)
+        col = lax.broadcasted_iota(jnp.int32, (128, d), 1)
+        for s in range(members):
+            place = jnp.where((col == row + s * own) & (row < own), 1.0, 0.0).astype(BF16)
+            total = total + nn(packs_ref[s // 4, s // 2 % 2, s % 2, 0:16, :], place)
+        vec_ref[...] = total[:8]
+        part = 3 * d // 2
+        gap = jnp.zeros((1, d // 2), F32)
+        biases = [jnp.concatenate([vec_ref[0:1, :], gap], 1), jnp.concatenate([gap, vec_ref[1:2, :]], 1)]
+
+        @pl.loop(0, n // tile)
+        def _(t):
+            r = pl.ds(pl.multiple_of(t * tile, tile), tile)
+            hat, _ = row_stats(x_ref[r, :].astype(F32))
+            n_ref[r, :] = (hat * vec_ref[4:5, :] + vec_ref[5:6, :]).astype(BF16)
+            for k in range(2):
+                w = w_ref[k * (nz // 2):(k + 1) * (nz // 2)].reshape(part, d)
+                qkv_ref[r, k * part:(k + 1) * part] = (nt(n_ref[r, :], w) + biases[k]).astype(BF16)
+            for k in range(n // tile):
+                if plan[k]:
+                    @pl.when(t == k)
+                    def _():
+                        for _, f, i in plan[k]:
+                            f(i)
+
+        pumped = plan[n // tile:]
+        low_half = pair_masks((n, 128))
+        half = pair_masks((tq, 128))
+        tiles = n // tq
+
+        @pl.loop(0, pairs)
+        def _(p):
+            def cols(k):
+                return pl.ds(pl.multiple_of(k * d + p * 128, 128), 128)
+
+            v = qkv_ref[:, cols(2)]
+            zero = jnp.zeros_like(v)
+            va[...] = jnp.where(low_half, v, zero)
+            vb[...] = jnp.where(low_half, zero, v)
+
+            @pl.loop(0, tiles)
+            def _(t):
+                r = pl.ds(pl.multiple_of(t * tq, tq), tq)
+                q = qkv_ref[r, cols(0)] * jnp.asarray(0.125, BF16)
+                qz = jnp.zeros_like(q)
+                kk = qkv_ref[:, cols(1)]
+                outs, tops, sums = [], [], []
+                for qh, vh in ((jnp.where(half, q, qz), va), (jnp.where(half, qz, q), vb)):
+                    s = nt(qh, kk) + mask[r, :]
+                    top = jnp.max(s, 1, keepdims=True)
+                    e = jnp.exp(s - top)
+                    sums.append(jnp.sum(e, 1, keepdims=True))
+                    tops.append(top)
+                    outs.append(nn(e.astype(BF16), vh[...]))
+                (la, lb), (ma, mb) = sums, tops
+                o_ref[r, cols(0)] = ((outs[0] + outs[1]) * jnp.where(half, 1.0 / la, 1.0 / lb)).astype(BF16)
+                lse = jnp.where(half, ma + jnp.log(la), mb + jnp.log(lb)).T
+                lse_ref[p, 0:1, r] = lse[0:1, :]
+                lse_ref[p, 1:2, r] = lse[64:65, :]
+                for k, step in enumerate(pumped):
+                    if step:
+                        @pl.when(p * tiles + t == k)
+                        def _():
+                            for _, f, i in step:
+                                f(i)
+
+        for _, f, i in events:
+            f(i)
+        g.leave()
+
+    vm = pl.BlockSpec(memory_space=pltpu.VMEM)
+    hbm = pl.BlockSpec(memory_space=pl.ANY)
+    sds = jax.ShapeDtypeStruct
+
+    def full(h, width):
+        return sds((nz, 2, 2, h, width), BF16)
+
+    outs = pl.pallas_call(
+        kernel,
+        out_shape=[sds((n, d), BF16), sds((n, 3 * d), BF16), sds((8, d), F32), sds((n, d), BF16),
+                   sds((pairs, 8, n), F32), full(pack.shape[0], 128)] + [full(h, d) for h in heights],
+        in_specs=[vm] * 9, out_specs=[vm] * 7 + [hbm] * 4,
+        scratch_shapes=[pltpu.VMEM((n, n), F32), pltpu.VMEM((n, 128), BF16), pltpu.VMEM((n, 128), BF16),
+                        pltpu.SemaphoreType.DMA((ni, 2 + nz)), pltpu.SemaphoreType.DMA((ni, 2 + nz)),
+                        pltpu.SemaphoreType.DMA((ni,))],
+        compiler_params=pltpu.CompilerParams(collective_id=0, has_side_effects=True, vmem_limit_bytes=60 << 20),
+        name="gather_attend",
+    )(tokens, seg_col, key_row, pack, *shards)
+    normed, qkv, vecs, mixed, lse, packs = outs[:6]
+    return (normed, qkv, vecs, mixed, lse.reshape(8 * pairs, n), packs.reshape(members, -1, 128),
+            [w.reshape(-1, d) for w in outs[6:]])
+
+
 def weight_grads_reduced(pairs, pack, shard_rows, cuts, blocks, nz, collective):
     nw = len(pairs)
     lefts = [a for ls, _ in pairs for a in ls]
@@ -766,40 +811,43 @@
      first_gain, first_shift, second_gain, second_shift, up_weight, up_bias, down_weight, down_bias,
      align_weight, align_bias, grad_output, grad_aligned) = args
     n, d = tokens.shape
-    shards = [qkv_weight.T, out_weight, up_weight.T, down_weight, align_weight.T]
     small = [query_bias, value_bias, out_bias, down_bias, first_gain, first_shift, second_gain, second_shift]
-    fast = mesh_shape["dp"] == 2 and mesh_shape["fsdp"] == 16
-    own = query_bias.shape[0]
-    pack = jnp.concatenate(small + [up_bias, align_bias])
-    pad = -pack.shape[0] % (48 * 128)
-    pack = jnp.pad(pack, (0, pad)).reshape(-1, 128)
-    gathered = gather_all(shards + [pack], fast)
-    qkv_t, out_w, up_t, down_w, align_t, packs = gathered
     members = mesh_shape["fsdp"]
-    packs = packs.reshape(members, -1).astype(F32)
-    vecs = packs[:, :8 * own].reshape(members, 8, own).transpose(1, 0, 2).reshape(8, d)
-    ub, ab = up_bias.shape[0], align_bias.shape[0]
-    up_b = packs[:, 8 * own:8 * own + ub].reshape(1, -1)
-    align_b = packs[:, 8 * own + ub:8 * own + ub + ab].reshape(1, -1)
-    qkv_b = jnp.concatenate([vecs[0:1], jnp.zeros((1, d), F32), vecs[1:2]], 1)
+    own, ub, ab = query_bias.shape[0], up_bias.shape[0], align_bias.shape[0]
+    ff, al = ub * members, ab * members
+    fast = mesh_shape["dp"] == 2 and members == 16
 
     seg = segment_ids[0]
     pad_row = padding[0]
     keys = jnp.where(pad_row == 0, seg, -1)
     valid_col = (1.0 - pad_row.astype(F32))[:, None]
-
-    def ranges(tile, block):
-        first = seg[::tile]
-        last = seg[tile - 1::tile]
-        lo = jnp.sum(seg[None, :] < first[:, None], 1, dtype=jnp.int32) // block
-        hi = (jnp.sum(seg[None, :] <= last[:, None], 1, dtype=jnp.int32) + block - 1) // block
-        return jnp.stack([lo, hi])
-
-    normed, qkv = project(tokens, vecs, qkv_b, qkv_t)
-    mixed, lse = attend(qkv, seg[:, None], keys[None, :], ranges(128, 256))
+    wins = windows(seg, 256)
+
+    if fast:
+        nz = members // 4
+        lines = [v[None] for v in small] + [up_bias[None, :128], up_bias[None, 128:], align_bias[None]]
+        pack = sum(jnp.pad(v, ((k, 47 - k), (0, 128 - v.shape[1]))) for k, v in enumerate(lines))
+        normed, qkv, vecs, mixed, lse, packs, full = gather_attend(
+            tokens, pack, [qkv_weight.T, out_weight, align_weight.T, up_weight.T, down_weight],
+            seg[:, None], keys[None, :], own, nz)
+        qkv_t, out_w, align_t, up_t, down_w = full
+        up_b = packs[:, 8:10].reshape(members, 256)[:, :ub].reshape(1, ff).astype(F32)
+        align_b = packs[:, 10, :ab].reshape(1, al).astype(F32)
+    else:
+        def gathered(a):
+            return lax.all_gather(a, "fsdp", axis=0, tiled=True)
+
+        qkv_t, out_w, up_t, down_w, align_t = [
+            gathered(a) for a in (qkv_weight.T, out_weight, up_weight.T, down_weight, align_weight.T)]
+        vecs = jnp.stack([gathered(v) for v in small]).astype(F32)
+        up_b = gathered(up_bias).astype(F32)[None]
+        align_b = gathered(align_bias).astype(F32)[None]
+        qkv_b = jnp.concatenate([vecs[0:1], jnp.zeros((1, d), F32), vecs[1:2]], 1)
+        normed, qkv = project(tokens, vecs, qkv_b, qkv_t)
+        mixed, lse = attend(qkv, seg[:, None], keys[None, :], wins)
     (n2, act, du, gb, block_out, aligned, res, rb, dm, s768, sff, sal) = middle(
         tokens, mixed, grad_output, grad_aligned, valid_col, vecs, up_b, align_b, out_w, up_t, down_w, align_t)
-    dq, dk, dv, bq, bv = attend_back(qkv, mixed, dm, lse, seg[None, :], keys[:, None], ranges(256, 256))
+    dq, dk, dv, bq, bv = attend_back(qkv, mixed, dm, lse, seg[None, :], keys[:, None], wins)
     grad_tokens, s1 = finish(tokens, res, dq, dk, dv, vecs, qkv_t)
 
     sums = jnp.concatenate(
@@ -810,7 +858,6 @@
     me = lax.axis_index("fsdp")
     pack = pack.reshape(-1)
     vec = lax.dynamic_slice(pack[:8 * d].reshape(8, d), (0, me * own), (8, own))
-    ff, al = up_t.shape[0], align_t.shape[0]
     g_ub = lax.dynamic_slice(pack, (8 * d + me * ub,), (ub,))
     g_ab = lax.dynamic_slice(pack, (8 * d + ff + me * ab,), (ab,))
     return (block_out, aligned, grad_tokens, g_qkv.T, vec[0], vec[1], g_out, vec[2], vec[4], vec[5], vec[6],

time: 414 us -> 338 us (0.82)
  Pallas kernels: 378 us -> 306 us
  local copies, waits for them, and re-layouts: 28.6 us -> 21.2 us
    pallas_call x5 -> x3, Pallas kernels: 193 us -> 107 us  [call(): pl.pallas_call(kernel, grid_spec=pltpu.PrefetchScalarGridSpec(num_scalar_...]
    pallas_call x1, Pallas kernels: 88.9 us -> 103 us  [gather_attend(): pl.pallas_call(kernel, out_shape=[sds((n, d), BF16), sds((n, 3 * d), BF16...]
    concatenate x2 -> x0, local copies, waits for them, and re-layouts: 6.76 us -> none  [the longest x1 6.75 us: per_device(): pack = jnp.concatenate(small + [up_bias, align_bias])]
where the time goes in v2:
time: 338 us; the launch traced here: 333 us
  Pallas kernels  306 us (91%)
  local copies, waits for them, and re-layouts  21.2 us (6%)
  other arithmetic  5.03 us (1%)
    pallas_call x3, Pallas kernels, call(): pl.pallas_call(kernel, grid_spec=pltpu.PrefetchScalarGridSpec(num_scalar_...  107 us
    pallas_call x1, Pallas kernels, gather_attend(): pl.pallas_call(kernel, out_shape=[sds((n, d), BF16), sds((n, 3 * d), BF16...  103 us
    pallas_call x1, Pallas kernels, weight_grads_reduced(): pl.pallas_call(kernel, out_shape=[jax.ShapeDtypeStruct((rw, width), F32)...  96.1 us

profile of v2, /device:TPU:0, one launch (start us, length us, event | category | flops | bytes accessed | tf_op | source)
XLA Modules:
  0.0 333.3 jit_solution(17574867789584384180)
XLA Ops:
  0.7 1.7 copy.44.sc_ref
  3.7 1.4 pad_add_fusion.p_ref
  5.1 1.3 compare_select_fusion.kr_ref
  6.4 102.9 %gather_attend.1 = (bf16[1024,768]{1,0:T(8,128)(2,1)}, bf16[1024,2304]{1,0:T(8,128)(2,1)}, f32[8,768]{1,0:T(8,128)}, bf16[1024,768]{1,0:T(8,128)(2,1)}, f32[6,8,...) custom-call(bf16[1024,768]{1,0:T(8,128)(2,1)} %x_ref.5, ...), custom_call_target="tpu_custom_call" | custom-call | tf_op jit(solution)/shard_map/gather_attend/pallas_call | solution.py:573
  109.3 0.8 slice.97
  110.8 0.8 slice.99
  112.3 1.0 copy.46.v_ref
  113.3 51.1 %middle.1 = (bf16[1024,768]{1,0:T(8,128)(2,1)}, bf16[1024,3072]{1,0:T(8,128)(2,1)}, bf16[1024,3072]{1,0:T(8,128)(2,1)}, bf16[1024,768]{1,0:T(8,128)(2,1)}, bf16[...) custom-call(bf16[1024,768]{1,0:T(8,128)(2,1)} %x_ref.5, ...), custom_call_target="tpu_custom_call" | custom-call | tf_op jit(solution)/shard_map/middle/pallas_call | solution.py:58
  165.8 0.8 broadcast_select_fusion.kc_ref
  166.6 45.8 %attend_back.1 = (bf16[1024,768]{1,0:T(8,128)(2,1)}, bf16[1024,768]{1,0:T(8,128)(2,1)}, bf16[1024,768]{1,0:T(8,128)(2,1)}, f32[8,768]{1,0:T(8,128)}, f32[8,768]{1,0:T(8,128)}) custom-call(s32[2,4]{1,0:T(2,128)} %pad_add_fusion.1.win, bf16[1024,2304]{1,0:T(8,128)(2,1)} %get-tuple-element.64.q_ref.k_ref.v_ref, ...), custom_call_target="tpu_custom_call" | custom-call | tf_op jit(solution)/shard_map/attend_back/pallas_call | solution.py:58
  212.4 10.2 %finish.1 = (bf16[1024,768]{1,0:T(8,128)(2,1)}, f32[8,768]{1,0:T(8,128)}) custom-call(bf16[1024,768]{1,0:T(8,128)(2,1)} %x_ref.5, f32[1024,768]{1,0:T(8,128)} %get-tuple-element.63.r_ref, bf16[1024,768]{1,0:T(8,128)(2,1)} %get-tuple-element.67.dq_ref.refs_4_, bf16[1024,768]{1,0:T(8,128)(2,1)} %get-tuple-element.68.dk_ref.refs_5_, ...), custom_call_target="tpu_custom_call" | custom-call | tf_op jit(solution)/shard_map/finish/pallas_call | solution.py:58
  222.6 0.7 slice.84
  223.4 0.7 slice.80
  224.1 0.7 slice.81
  224.9 0.9 slice.86
  225.8 0.8 slice.87
  227.2 96.1 %reduce_grads.1 = (f32[64,768]{1,0:T(8,128)}, f32[192,768]{1,0:T(8,128)}, f32[192,768]{1,0:T(8,128)}, f32[48,768]{1,0:T(8,128)}, f32[144,768]{1,0:T(8,128)}, /*index=5*/f32[80,128]{1,0:T(8,128)}) custom-call(bf16[1024,1024]{1,0:T(8,128)(2,1)} %refs_0_.1, bf16[1024,3072]{1,0:T(8,128)(2,1)} %get-tuple-element.72.refs_1_, ...), custom_call_target="tpu_custom_call" | custom-call | tf_op jit(solution)/shard_map/reduce_grads/pallas_call | solution.py:785
  323.4 0.8 slice.88
  324.8 1.3 dynamic_slice.10
  326.2 1.3 dynamic_slice.11
  327.4 1.8 copy.59
  329.3 1.6 copy.60
  330.8 0.8 copy.61
  331.7 0.8 copy.62
  (38 shorter events, 6.0 us)
Async XLA Ops:
  6.4 105.9 %copy-start.5 = (s32[1,1024]{1,0:T(1,128)S(1)}, s32[1,1024]{1,0:T(1,128)}, u32[]{:S(2)}) copy-start(s32[1,1024]{1,0:T(1,128)} %param.22) | copy-start | bytes 12292
  113.3 51.2 %copy-start.4 = (s32[1,1024]{1,0:T(1,128)S(1)}, s32[1,1024]{1,0:T(1,128)}, u32[]{:S(2)}) copy-start(s32[1,1024]{1,0:T(1,128)} %sr_ref.1) | copy-start | bytes 12292
  113.3 52.5 %copy-start = (s32[1024,1]{1,0:T(8,128)S(1)}, s32[1024,1]{1,0:T(8,128)}, u32[]{:S(2)}) copy-start(s32[1024,1]{1,0:T(8,128)} %copy.44.sc_ref) | copy-start | bytes 12292
  212.4 12.5 %copy-start.6 = (f32[8,768]{1,0:T(8,128)S(1)}, f32[8,768]{1,0:T(8,128)}, u32[]{:S(2)}) copy-start(f32[8,768]{1,0:T(8,128)} %get-tuple-element.80) | copy-start | bytes 73732
  323.3 7.5 %copy-start.2 = (f32[192,768]{1,0:T(8,128)S(1)}, f32[192,768]{1,0:T(8,128)}, u32[]{:S(2)}) copy-start(f32[192,768]{1,0:T(8,128)} %get-tuple-element.87) | copy-start | bytes 1769476
  323.4 8.3 %copy-start.1 = (f32[192,768]{1,0:T(8,128)S(1)}, f32[192,768]{1,0:T(8,128)}, u32[]{:S(2)}) copy-start(f32[192,768]{1,0:T(8,128)} %get-tuple-element.136) | copy-start | bytes 1769476
  327.4 5.1 %copy-start.3 = (f32[64,768]{1,0:T(8,128)S(1)}, f32[64,768]{1,0:T(8,128)}, u32[]{:S(2)}) copy-start(f32[64,768]{1,0:T(8,128)} %get-tuple-element.89) | copy-start | bytes 589828

commit v3 on v2

--- a/solution.py
+++ b/solution.py
@@ -256,7 +256,7 @@
 
 
 def middle(tokens, mixed, grad_output, grad_aligned, valid_col, vecs, up_b, align_b,
-           out_w, up_t, down_w, align_t, tile=512, chunk=768):
+           out_w, up_t, down_w, align_t, tile=256, chunk=768):
     n, d = tokens.shape
     ff, al = up_t.shape[0], align_t.shape[0]
 
@@ -586,7 +586,7 @@
             [w.reshape(-1, d) for w in outs[6:]])
 
 
-def weight_grads_reduced(pairs, pack, shard_rows, cuts, blocks, nz, collective):
+def finish_and_reduce(pairs, tokens, resid_grad, vecs, qkv_t, sums, shard_rows, cuts, blocks, nz, collective, tile=256):
     nw = len(pairs)
     lefts = [a for ls, _ in pairs for a in ls]
     rights = [r for _, r in pairs]
@@ -600,10 +600,14 @@
         left_refs = refs[:len(lefts)]
         right_refs = refs[len(lefts):len(lefts) + nw]
         pos = len(lefts) + nw
-        pack_ref = refs[pos]
-        out_refs = refs[pos + 1:pos + 1 + nw]
-        pack_out = refs[pos + 1 + nw]
+        x_hbm, r_hbm, w_hbm, vec_ref = refs[pos:pos + 4]
+        sum_refs = refs[pos + 4:pos + 9]
+        pos += 9
+        out_refs = refs[pos:pos + nw]
+        pack_out, g_hbm = refs[pos + nw:pos + nw + 2]
         pos += 2 + nw
+        x_ref, r_ref, w_ref, s1_ref, fsem = refs[pos:pos + 5]
+        pos += 5
         lbuf, rbuf = refs[pos:pos + 2]
         part, sibb, yb, xb, zb, fin, finb = [refs[pos + 2 + k * nw:pos + 2 + (k + 1) * nw] for k in range(7)]
         pos += 2 + 7 * nw
@@ -669,12 +673,15 @@
                     cp.wait()
             cols = pl.ds(j * lb, lb)
             right = rbuf[w % 2, :, cols]
-            for half in range(nz // 2):
-                left = lbuf[w % 2, :, pl.ds(half * 8 * rw, 8 * rw)]
+
+            @pl.loop(0, nz // 2)
+            def _(half):
+                left = lbuf[w % 2, :, pl.ds(pl.multiple_of(half * 8 * rw, 128), 8 * rw)]
                 g = tn(left, right).astype(BF16)
                 for k in range(8):
                     part[w][j, k % 2, (k // 2) % 2, 2 * half + k // 4] = g[k * rw:(k + 1) * rw]
-            if j == width // lb - 1 and w + 2 < nw:
+
+            if w > 0 and j == width // lb - 1 and w + 2 < nw:
                 load(w + 2)
             flight[i, 0] = send(i, 0, part[w].at[j, 1 - c], sibb[w].at[j], sib)
 
@@ -682,9 +689,12 @@
             w, j = items[i]
             flight[i, 0].wait_recv()
             mine = part[w].at[j, c]
-            for xx in range(2):
-                for zz in range(nz):
+
+            @pl.loop(0, nz)
+            def _(zz):
+                for xx in range(2):
                     mine[xx, zz] = (mine[xx, zz].astype(F32) + sibb[w][j, xx, zz].astype(F32)).astype(BF16)
+
             flight[i, 1] = send(i, 1, mine.at[:, :, rows_of(w, "theirs")], yb[w].at[j], yn)
 
         def stage_y(i):
@@ -692,9 +702,12 @@
             flight[i, 1].wait_recv()
             mine = part[w].at[j, c]
             r = rows_of(w, "mine")
-            for xx in range(2):
-                for zz in range(nz):
+
+            @pl.loop(0, nz)
+            def _(zz):
+                for xx in range(2):
                     mine[xx, zz, r] = (mine[xx, zz, r].astype(F32) + yb[w][j, xx, zz].astype(F32)).astype(BF16)
+
             flight[i, 2] = send(i, 2, mine.at[1 - x, :, rows_of(w, "plane")], xb[w].at[j], xn)
 
         def stage_x(i):
@@ -702,8 +715,11 @@
             flight[i, 2].wait_recv()
             mine = part[w].at[j, c, x]
             r = rows_of(w, "plane")
-            for zz in range(nz):
+
+            @pl.loop(0, nz)
+            def _(zz):
                 mine[zz, r] = (mine[zz, r].astype(F32) + xb[w][j, zz].astype(F32)).astype(BF16)
+
             for d in range(1, nz):
                 flight[i, 2 + d] = send(i, 2 + d, mine.at[zp[d], r], zb[w].at[j, d - 1], zd[d])
 
@@ -740,7 +756,9 @@
                 pack_cp[k - 1].wait()
                 pbuf[0, k] = pbuf[0, k - 1] + pbuf[1, k - 1]
             else:
-                pbuf[0, 0] = pack_ref[...]
+                pbuf[0, 0] = jnp.zeros_like(pbuf[0, 0])
+                for row, col, value in sum_rows(s1_ref[...], *[ref[...] for ref in sum_refs]):
+                    pbuf[0, 0, row:row + 1, 0:col] = value
             if k < len(pack_to):
                 cp = pltpu.make_async_remote_copy(
                     src_ref=pbuf.at[0, k], dst_ref=pbuf.at[1, k], send_sem=psem.at[k], recv_sem=prsem.at[k],
@@ -750,7 +768,39 @@
             else:
                 pack_out[...] = pbuf[0, k]
 
+        tiles = n // tile
+        held = [pltpu.make_async_copy(w_hbm, w_ref, fsem.at[0]), pltpu.make_async_copy(x_hbm, x_ref, fsem.at[1])]
+        written = []
+
+        def resid(k):
+            return pltpu.make_async_copy(r_hbm.at[pl.ds(k * tile, tile)], r_ref.at[k % 2], fsem.at[2 + tiles + k])
+
+        def finish_tile(k):
+            if k == 0:
+                s1_ref[...] = jnp.zeros_like(s1_ref)
+                for cp in held:
+                    cp.wait()
+            r = pl.ds(k * tile, tile)
+            resid(k).wait()
+            dn = nn(lbuf[0, r, 0:width], w_ref[0:width, :])
+            for part in range(1, 3):
+                span = slice(part * width, (part + 1) * width)
+                dn = dn + nn(lbuf[0, r, span], w_ref[span, :])
+            hat, rstd = row_stats(x_ref[r, :].astype(F32))
+            x_ref[r, :] = (r_ref[k % 2] + norm_back(dn * vec_ref[4:5, :], hat, rstd)).astype(BF16)
+            if k + 2 < tiles:
+                resid(k + 2).start()
+            s1_ref[0:1, :] += col_sum(dn * hat)
+            s1_ref[1:2, :] += col_sum(dn)
+            cp = pltpu.make_async_copy(x_ref.at[r], g_hbm.at[r], fsem.at[2 + k])
+            cp.start()
+            written.append(cp)
+            if k == tiles - 1:
+                load(2)
+
         load(0)
+        for cp in held + [resid(0), resid(1)]:
+            cp.start()
         load(1)
         pl.semaphore_wait(barrier, len(peers))
         stages = [compute, stage_sib, stage_y, stage_x, stage_z, stage_out]
@@ -758,10 +808,14 @@
             for k, stage in enumerate(stages):
                 if 0 <= t - k < ni:
                     stage(t - k)
-            if t <= len(pack_to):
-                pack_step(t)
+            if t < tiles:
+                finish_tile(t)
+            elif t - tiles <= len(pack_to):
+                pack_step(t - tiles)
         for cp in started:
             cp.wait_send()
+        for cp in written:
+            cp.wait()
 
     any_spec = pl.BlockSpec(memory_space=pl.ANY)
     vm = pl.BlockSpec(memory_space=pltpu.VMEM)
@@ -769,7 +823,10 @@
     def per_weight(make):
         return [pltpu.VMEM(make(width // b, shard_rows[w], cuts[w], b), BF16) for w, b in enumerate(blocks)]
 
-    scratch = [pltpu.VMEM((2, n, max_left), BF16), pltpu.VMEM((2, n, width), BF16)]
+    tiles = n // tile
+    scratch = [pltpu.VMEM((n, width), BF16), pltpu.VMEM((2, tile, width), F32), pltpu.VMEM(qkv_t.shape, BF16),
+               pltpu.VMEM((8, width), F32), pltpu.SemaphoreType.DMA((2 + 2 * tiles,)),
+               pltpu.VMEM((2, n, max_left), BF16), pltpu.VMEM((2, n, width), BF16)]
     scratch += per_weight(lambda j, rw, a, b: (j, 2, 2, nz, rw, b))
     scratch += per_weight(lambda j, rw, a, b: (j, 2, nz, rw, b))
     scratch += per_weight(lambda j, rw, a, b: (j, 2, nz, a, b))
@@ -778,34 +835,45 @@
     scratch += per_weight(lambda j, rw, a, b: (j, rw - a, b))
     scratch += per_weight(lambda j, rw, a, b: (j, rw - a, b))
     scratch += [
-        pltpu.VMEM((2, 6) + pack.shape, F32),
+        pltpu.VMEM((2, 6, 16, 1024), F32),
         pltpu.SemaphoreType.DMA((ni, 3 + nz)), pltpu.SemaphoreType.DMA((ni, 3 + nz)),
         pltpu.SemaphoreType.DMA((6,)), pltpu.SemaphoreType.DMA((6,)), pltpu.SemaphoreType.DMA((nw, 4)),
     ]
     outs = pl.pallas_call(
         kernel,
         out_shape=[jax.ShapeDtypeStruct((rw, width), F32) for rw in shard_rows]
-        + [jax.ShapeDtypeStruct(pack.shape, F32)],
-        in_specs=[any_spec] * (len(lefts) + nw) + [vm],
-        out_specs=[vm] * (nw + 1),
+        + [jax.ShapeDtypeStruct((16, 1024), F32), jax.ShapeDtypeStruct((n, width), BF16)],
+        in_specs=[any_spec] * (len(lefts) + nw + 3) + [vm] * 6,
+        out_specs=[vm] * (nw + 1) + [any_spec],
         scratch_shapes=scratch,
         compiler_params=pltpu.CompilerParams(
             collective_id=collective, has_side_effects=True, vmem_limit_bytes=63 << 20),
-        name="reduce_grads",
-    )(*lefts, *rights, pack)
-    return outs[:nw], outs[nw]
-
-
-def reduce_all(pairs, pack, fast):
+        name="finish_reduce",
+    )(*lefts, *rights, tokens, resid_grad, qkv_t, vecs, *sums)
+    return outs[:nw], outs[nw], outs[nw + 1]
+
+
+def sum_rows(s1, bq, bv, s768, sff, sal):
+    lines = [bq[0:1], bv[0:1], s768[1:2], s768[0:1], s1[0:1], s1[1:2], s768[2:3], s768[3:4], sal[0:1]]
+    lines += [sff[0:1, k:k + 1024] for k in range(0, sff.shape[1], 1024)]
+    return [(row, v.shape[1], v) for row, v in enumerate(lines)]
+
+
+def reduce_all(pairs, tokens, resid_grad, vecs, qkv_t, sums, fast):
     if fast:
         left_rows = [sum(a.shape[1] for a in ls) for ls, _ in pairs]
         shard_rows = [r // 16 for r in left_rows]
         cuts = [max(16, (r * 5 // 16) // 16 * 16) for r in shard_rows]
-        blocks = [384, 256, 256, 768, 256]
-        return weight_grads_reduced(pairs, pack, shard_rows, cuts, blocks, 4, 1)
+        blocks = [256, 256, 256, 384, 384]
+        return finish_and_reduce(pairs, tokens, resid_grad, vecs, qkv_t, sums, shard_rows, cuts, blocks, 4, 1)
+    grad_tokens, s1 = finish(tokens, resid_grad, *pairs[0][0], vecs, qkv_t)
     terms = [jnp.concatenate([tn(a, r).astype(BF16) for a in ls], 0) for ls, r in pairs]
     got = [lax.psum(lax.psum_scatter(t, "fsdp", scatter_dimension=0, tiled=True), "dp").astype(F32) for t in terms]
-    return got, lax.psum(pack, ("dp", "fsdp"))
+    lines = [jnp.pad(v, ((0, 0), (0, 1024 - k))) for _, k, v in sum_rows(s1, *sums)]
+    pack = jnp.pad(jnp.concatenate(lines, 0), ((0, 16 - len(lines)), (0, 0)))
+    return got, lax.psum(pack, ("dp", "fsdp")), grad_tokens
+
+
 def per_device(mesh_shape, *args):
     (tokens, segment_ids, padding, qkv_weight, query_bias, value_bias, out_weight, out_bias,
      first_gain, first_shift, second_gain, second_shift, up_weight, up_bias, down_weight, down_bias,
@@ -848,18 +916,13 @@
     (n2, act, du, gb, block_out, aligned, res, rb, dm, s768, sff, sal) = middle(
         tokens, mixed, grad_output, grad_aligned, valid_col, vecs, up_b, align_b, out_w, up_t, down_w, align_t)
     dq, dk, dv, bq, bv = attend_back(qkv, mixed, dm, lse, seg[None, :], keys[:, None], wins)
-    grad_tokens, s1 = finish(tokens, res, dq, dk, dv, vecs, qkv_t)
-
-    sums = jnp.concatenate(
-        [bq[0:1], bv[0:1], s768[1:2], s768[0:1], s1[0:2], s768[2:4]], 0)
-    pack = jnp.concatenate([sums.reshape(-1), sff[0], sal[0]]).reshape(-1, 128)
-    pairs = [([grad_aligned], block_out), ([act], gb), ([du], n2), ([mixed], rb), ([dq, dk, dv], normed)]
-    (g_align, g_down, g_up, g_out, g_qkv), pack = reduce_all(pairs, pack, fast)
+    pairs = [([dq, dk, dv], normed), ([act], gb), ([du], n2), ([mixed], rb), ([grad_aligned], block_out)]
+    (g_qkv, g_down, g_up, g_out, g_align), pack, grad_tokens = reduce_all(
+        pairs, tokens, res, vecs, qkv_t, (bq, bv, s768, sff, sal), fast)
     me = lax.axis_index("fsdp")
-    pack = pack.reshape(-1)
-    vec = lax.dynamic_slice(pack[:8 * d].reshape(8, d), (0, me * own), (8, own))
-    g_ub = lax.dynamic_slice(pack, (8 * d + me * ub,), (ub,))
-    g_ab = lax.dynamic_slice(pack, (8 * d + ff + me * ab,), (ab,))
+    vec = lax.dynamic_slice(pack, (0, me * own), (8, own))
+    g_ub = lax.dynamic_slice(pack[9:9 + ff // 1024].reshape(ff), (me * ub,), (ub,))
+    g_ab = lax.dynamic_slice(pack[8], (me * ab,), (ab,))
     return (block_out, aligned, grad_tokens, g_qkv.T, vec[0], vec[1], g_out, vec[2], vec[4], vec[5], vec[6],
             vec[7], g_up.T, g_ub, g_down, vec[3], g_align.T, g_ab)
 

time: 338 us -> 332 us (0.982); the launches traced: 333 us -> 332 us
    pallas_call x1, Pallas kernels: 96.1 us -> 108 us  [finish_and_reduce(): pl.pallas_call(kernel, out_shape=[jax.ShapeDtypeStruct((rw, width), F32)...]
    pallas_call x3 -> x2, Pallas kernels: 107 us -> 98.3 us  [call(): pl.pallas_call(kernel, grid_spec=pltpu.PrefetchScalarGridSpec(num_scalar_...]
where the time goes in v3:
time: 332 us
  Pallas kernels  309 us (93%)
  local copies, waits for them, and re-layouts  18 us (5%)
  other arithmetic  4.41 us (1%)
    pallas_call x1, Pallas kernels, finish_and_reduce(): pl.pallas_call(kernel, out_shape=[jax.ShapeDtypeStruct((rw, width), F32)...  108 us
    pallas_call x1, Pallas kernels, gather_attend(): pl.pallas_call(kernel, out_shape=[sds((n, d), BF16), sds((n, 3 * d), BF16...  103 us
    pallas_call x2, Pallas kernels, call(): pl.pallas_call(kernel, grid_spec=pltpu.PrefetchScalarGridSpec(num_scalar_...  98.3 us

profile of v3, /device:TPU:0, one launch (start us, length us, event | category | flops | bytes accessed | tf_op | source)
XLA Modules:
  0.0 332.3 jit_solution(3313662741014465561)
XLA Ops:
  0.7 1.7 copy.44.sc_ref
  2.4 0.7 slice_bitcast_fusion.8
  3.0 0.7 slice_bitcast_fusion.9
  3.7 1.4 pad_add_fusion.p_ref
  5.1 1.3 compare_select_fusion.kr_ref
  6.4 102.9 %gather_attend.1 = (bf16[1024,768]{1,0:T(8,128)(2,1)}, bf16[1024,2304]{1,0:T(8,128)(2,1)}, f32[8,768]{1,0:T(8,128)}, bf16[1024,768]{1,0:T(8,128)(2,1)}, f32[6,8,...) custom-call(bf16[1024,768]{1,0:T(8,128)(2,1)} %refs_12_.1, ...), custom_call_target="tpu_custom_call" | custom-call | tf_op jit(solution)/shard_map/gather_attend/pallas_call | solution.py:573
  109.3 0.8 slice.68
  110.1 0.7 reshape.266.ub_ref
  110.8 0.8 slice.70
  111.6 0.7 reshape.267.ab_ref
  112.2 1.0 copy.46.v_ref
  113.3 52.6 %middle.1 = (bf16[1024,768]{1,0:T(8,128)(2,1)}, bf16[1024,3072]{1,0:T(8,128)(2,1)}, bf16[1024,3072]{1,0:T(8,128)(2,1)}, bf16[1024,768]{1,0:T(8,128)(2,1)}, bf16[...) custom-call(bf16[1024,768]{1,0:T(8,128)(2,1)} %refs_12_.1, ...), custom_call_target="tpu_custom_call" | custom-call | tf_op jit(solution)/shard_map/middle/pallas_call | solution.py:58
  167.2 0.8 broadcast_select_fusion.kc_ref
  168.0 45.7 %attend_back.1 = (bf16[1024,768]{1,0:T(8,128)(2,1)}, bf16[1024,768]{1,0:T(8,128)(2,1)}, bf16[1024,768]{1,0:T(8,128)(2,1)}, f32[8,768]{1,0:T(8,128)}, f32[8,768]{1,0:T(8,128)}) custom-call(s32[2,4]{1,0:T(2,128)} %pad_add_fusion.1.win, bf16[1024,2304]{1,0:T(8,128)(2,1)} %get-tuple-element.62.q_ref.k_ref.v_ref, ...), custom_call_target="tpu_custom_call" | custom-call | tf_op jit(solution)/shard_map/attend_back/pallas_call | solution.py:58
  213.8 107.9 %finish_reduce.1 = (f32[144,768]{1,0:T(8,128)}, f32[192,768]{1,0:T(8,128)}, f32[192,768]{1,0:T(8,128)}, f32[48,768]{1,0:T(8,128)}, f32[64,768]{1,0:T(8,128)}, /*...) custom-call(bf16[1024,768]{1,0:T(8,128)(2,1)} %get-tuple-element.65.refs_0_, bf16[1024,768]{1,0:T(8,128)(2,1)} %get-tuple-element.66.refs_1_, ...), custom_call_target="tpu_custom_call" | custom-call | tf_op jit(solution)/shard_map/finish_reduce/pallas_call | solution.py:842
  321.7 0.8 slice.65
  323.1 0.8 constant_dynamic-slice_fusion
  324.5 0.8 slice.67
  325.8 2.7 copy.60
  328.6 0.8 copy.61
  329.3 0.7 copy.62
  330.0 0.8 copy.63
  330.8 0.8 copy.64
  331.6 0.7 copy.65
  (31 shorter events, 3.1 us)
Async XLA Ops:
  6.4 105.8 %copy-start.7 = (s32[1,1024]{1,0:T(1,128)S(1)}, s32[1,1024]{1,0:T(1,128)}, u32[]{:S(2)}) copy-start(s32[1,1024]{1,0:T(1,128)} %param.22) | copy-start | bytes 12292
  113.3 52.6 %copy-start.6 = (s32[1,1024]{1,0:T(1,128)S(1)}, s32[1,1024]{1,0:T(1,128)}, u32[]{:S(2)}) copy-start(s32[1,1024]{1,0:T(1,128)} %sr_ref.1) | copy-start | bytes 12292
  113.3 53.9 %copy-start = (s32[1024,1]{1,0:T(8,128)S(1)}, s32[1024,1]{1,0:T(8,128)}, u32[]{:S(2)}) copy-start(s32[1024,1]{1,0:T(8,128)} %copy.44.sc_ref) | copy-start | bytes 12292
  325.8 2.8 copy-start.3
  325.8 3.5 %copy-start.5 = (f32[48,768]{1,0:T(8,128)S(1)}, f32[48,768]{1,0:T(8,128)}, u32[]{:S(2)}) copy-start(f32[48,768]{1,0:T(8,128)} %get-tuple-element.124) | copy-start | bytes 442372
  325.8 4.2 %copy-start.2 = (f32[192,768]{1,0:T(8,128)S(1)}, f32[192,768]{1,0:T(8,128)}, u32[]{:S(2)}) copy-start(f32[192,768]{1,0:T(8,128)} %get-tuple-element.85) | copy-start | bytes 1769476
  328.5 2.3 copy-start.1
  328.6 3.1 copy-start.4

commit v4 on v3

--- a/solution.py
+++ b/solution.py
@@ -586,7 +586,21 @@
             [w.reshape(-1, d) for w in outs[6:]])
 
 
-def finish_and_reduce(pairs, tokens, resid_grad, vecs, qkv_t, sums, shard_rows, cuts, blocks, nz, collective, tile=256):
+def plan_steps(count, tiles, first_tile, hops, lags):
+    steps = []
+    for t in range(max(count + max(lags), first_tile + tiles + hops + 1)):
+        stages = [(t - lag, kind) for kind, lag in zip(("compute", "sib", "y", "x", "z", "out"), (0,) + lags)]
+        steps += [(kind, i) for i, kind in stages if 0 <= i < count]
+        k = t - first_tile
+        if 0 <= k < tiles:
+            steps.append(("finish", k))
+        elif 0 <= k - tiles <= hops:
+            steps.append(("pack", k - tiles))
+    return steps
+
+
+def finish_and_reduce(pairs, tokens, resid_grad, vecs, qkv_t, sums, shard_rows, cuts, blocks, nz, collective, tile=256,
+                      qkv=2, first_tile=7, lags=(1, 2, 4, 6, 7)):
     nw = len(pairs)
     lefts = [a for ls, _ in pairs for a in ls]
     rights = [r for _, r in pairs]
@@ -595,6 +609,8 @@
     max_left = max(sum(a.shape[1] for a in ls) for ls, _ in pairs)
     items = [(w, j) for w in range(nw) for j in range(width // blocks[w])]
     ni = len(items)
+    first_tile = max(max(i for i, (w, _) in enumerate(items) if w == qkv), first_tile)
+    steps = plan_steps(ni, n // tile, first_tile, 5, lags)
 
     def kernel(*refs):
         left_refs = refs[:len(lefts)]
@@ -681,7 +697,7 @@
                 for k in range(8):
                     part[w][j, k % 2, (k // 2) % 2, 2 * half + k // 4] = g[k * rw:(k + 1) * rw]
 
-            if w > 0 and j == width // lb - 1 and w + 2 < nw:
+            if w != qkv and j == width // lb - 1 and w + 2 < nw:
                 load(w + 2)
             flight[i, 0] = send(i, 0, part[w].at[j, 1 - c], sibb[w].at[j], sib)
 
@@ -782,10 +798,10 @@
                     cp.wait()
             r = pl.ds(k * tile, tile)
             resid(k).wait()
-            dn = nn(lbuf[0, r, 0:width], w_ref[0:width, :])
+            dn = nn(lbuf[qkv % 2, r, 0:width], w_ref[0:width, :])
             for part in range(1, 3):
                 span = slice(part * width, (part + 1) * width)
-                dn = dn + nn(lbuf[0, r, span], w_ref[span, :])
+                dn = dn + nn(lbuf[qkv % 2, r, span], w_ref[span, :])
             hat, rstd = row_stats(x_ref[r, :].astype(F32))
             x_ref[r, :] = (r_ref[k % 2] + norm_back(dn * vec_ref[4:5, :], hat, rstd)).astype(BF16)
             if k + 2 < tiles:
@@ -796,22 +812,17 @@
             cp.start()
             written.append(cp)
             if k == tiles - 1:
-                load(2)
+                load(qkv + 2)
 
         load(0)
+        load(1)
         for cp in held + [resid(0), resid(1)]:
             cp.start()
-        load(1)
         pl.semaphore_wait(barrier, len(peers))
-        stages = [compute, stage_sib, stage_y, stage_x, stage_z, stage_out]
-        for t in range(ni + len(stages) - 1):
-            for k, stage in enumerate(stages):
-                if 0 <= t - k < ni:
-                    stage(t - k)
-            if t < tiles:
-                finish_tile(t)
-            elif t - tiles <= len(pack_to):
-                pack_step(t - tiles)
+        does = {"compute": compute, "sib": stage_sib, "y": stage_y, "x": stage_x, "z": stage_z, "out": stage_out,
+                "finish": finish_tile, "pack": pack_step}
+        for kind, i in steps:
+            does[kind](i)
         for cp in started:
             cp.wait_send()
         for cp in written:
@@ -864,9 +875,9 @@
         left_rows = [sum(a.shape[1] for a in ls) for ls, _ in pairs]
         shard_rows = [r // 16 for r in left_rows]
         cuts = [max(16, (r * 5 // 16) // 16 * 16) for r in shard_rows]
-        blocks = [256, 256, 256, 384, 384]
+        blocks = [384, 256, 256, 256, 384]
         return finish_and_reduce(pairs, tokens, resid_grad, vecs, qkv_t, sums, shard_rows, cuts, blocks, 4, 1)
-    grad_tokens, s1 = finish(tokens, resid_grad, *pairs[0][0], vecs, qkv_t)
+    grad_tokens, s1 = finish(tokens, resid_grad, *pairs[2][0], vecs, qkv_t)
     terms = [jnp.concatenate([tn(a, r).astype(BF16) for a in ls], 0) for ls, r in pairs]
     got = [lax.psum(lax.psum_scatter(t, "fsdp", scatter_dimension=0, tiled=True), "dp").astype(F32) for t in terms]
     lines = [jnp.pad(v, ((0, 0), (0, 1024 - k))) for _, k, v in sum_rows(s1, *sums)]
@@ -916,8 +927,8 @@
     (n2, act, du, gb, block_out, aligned, res, rb, dm, s768, sff, sal) = middle(
         tokens, mixed, grad_output, grad_aligned, valid_col, vecs, up_b, align_b, out_w, up_t, down_w, align_t)
     dq, dk, dv, bq, bv = attend_back(qkv, mixed, dm, lse, seg[None, :], keys[:, None], wins)
-    pairs = [([dq, dk, dv], normed), ([act], gb), ([du], n2), ([mixed], rb), ([grad_aligned], block_out)]
-    (g_qkv, g_down, g_up, g_out, g_align), pack, grad_tokens = reduce_all(
+    pairs = [([grad_aligned], block_out), ([act], gb), ([dq, dk, dv], normed), ([du], n2), ([mixed], rb)]
+    (g_align, g_down, g_qkv, g_up, g_out), pack, grad_tokens = reduce_all(
         pairs, tokens, res, vecs, qkv_t, (bq, bv, s768, sff, sal), fast)
     me = lax.axis_index("fsdp")
     vec = lax.dynamic_slice(pack, (0, me * own), (8, own))

time: 332 us -> 324 us (0.976)
  Pallas kernels: 309 us -> 301 us
    pallas_call x2, Pallas kernels: 98.3 us -> 89.5 us  [call(): pl.pallas_call(kernel, grid_spec=pltpu.PrefetchScalarGridSpec(num_scalar_...]
where the time goes in v4:
time: 324 us
  Pallas kernels  301 us (93%)
  local copies, waits for them, and re-layouts  18 us (6%)
  other arithmetic  4.41 us (1%)
    pallas_call x1, Pallas kernels, finish_and_reduce(): pl.pallas_call(kernel, out_shape=[jax.ShapeDtypeStruct((rw, width), F32)...  109 us
    pallas_call x1, Pallas kernels, gather_attend(): pl.pallas_call(kernel, out_shape=[sds((n, d), BF16), sds((n, 3 * d), BF16...  103 us
    pallas_call x2, Pallas kernels, call(): pl.pallas_call(kernel, grid_spec=pltpu.PrefetchScalarGridSpec(num_scalar_...  89.5 us
    unnamed x23, local copies, waits for them, and re-layouts  6.51 us

profile of v4, /device:TPU:0, one launch (start us, length us, event | category | flops | bytes accessed | tf_op | source)
XLA Modules:
  0.0 324.1 jit_solution(14593429036470042483)
XLA Ops:
  0.7 1.7 copy.44.sc_ref
  2.4 0.7 slice_bitcast_fusion.8
  3.0 0.7 slice_bitcast_fusion.9
  3.7 1.4 pad_add_fusion.p_ref
  5.1 1.3 compare_select_fusion.kr_ref
  6.4 102.9 %gather_attend.1 = (bf16[1024,768]{1,0:T(8,128)(2,1)}, bf16[1024,2304]{1,0:T(8,128)(2,1)}, f32[8,768]{1,0:T(8,128)}, bf16[1024,768]{1,0:T(8,128)(2,1)}, f32[6,8,...) custom-call(bf16[1024,768]{1,0:T(8,128)(2,1)} %refs_12_.1, ...), custom_call_target="tpu_custom_call" | custom-call | tf_op jit(solution)/shard_map/gather_attend/pallas_call | solution.py:573
  109.3 0.8 slice.68
  110.1 0.7 reshape.266.ub_ref
  110.8 0.8 slice.70
  111.6 0.7 reshape.267.ab_ref
  112.2 1.0 copy.46.v_ref
  113.3 52.6 %middle.1 = (bf16[1024,768]{1,0:T(8,128)(2,1)}, bf16[1024,3072]{1,0:T(8,128)(2,1)}, bf16[1024,3072]{1,0:T(8,128)(2,1)}, bf16[1024,768]{1,0:T(8,128)(2,1)}, bf16[...) custom-call(bf16[1024,768]{1,0:T(8,128)(2,1)} %refs_12_.1, ...), custom_call_target="tpu_custom_call" | custom-call | tf_op jit(solution)/shard_map/middle/pallas_call | solution.py:58
  167.2 0.8 broadcast_select_fusion.kc_ref
  168.0 36.9 %attend_back.1 = (bf16[1024,768]{1,0:T(8,128)(2,1)}, bf16[1024,768]{1,0:T(8,128)(2,1)}, bf16[1024,768]{1,0:T(8,128)(2,1)}, f32[8,768]{1,0:T(8,128)}, f32[8,768]{1,0:T(8,128)}) custom-call(s32[2,4]{1,0:T(2,128)} %pad_add_fusion.1.win, bf16[1024,2304]{1,0:T(8,128)(2,1)} %get-tuple-element.63.q_ref.k_ref.v_ref, ...), custom_call_target="tpu_custom_call" | custom-call | tf_op jit(solution)/shard_map/attend_back/pallas_call | solution.py:58
  204.9 108.6 %finish_reduce.1 = (f32[64,768]{1,0:T(8,128)}, f32[192,768]{1,0:T(8,128)}, f32[144,768]{1,0:T(8,128)}, f32[192,768]{1,0:T(8,128)}, f32[48,768]{1,0:T(8,128)}, /*...) custom-call(bf16[1024,1024]{1,0:T(8,128)(2,1)} %refs_0_.1, bf16[1024,3072]{1,0:T(8,128)(2,1)} %get-tuple-element.62.refs_1_, ...), custom_call_target="tpu_custom_call" | custom-call | tf_op jit(solution)/shard_map/finish_reduce/pallas_call | solution.py:853
  313.5 0.8 slice.65
  314.9 0.8 constant_dynamic-slice_fusion
  316.3 0.8 slice.67
  317.6 2.7 copy.60
  320.4 0.8 copy.61
  321.1 0.7 copy.62
  321.8 0.8 copy.63
  322.6 0.8 copy.64
  323.4 0.7 copy.65
  (31 shorter events, 3.1 us)
Async XLA Ops:
  6.4 105.8 %copy-start.7 = (s32[1,1024]{1,0:T(1,128)S(1)}, s32[1,1024]{1,0:T(1,128)}, u32[]{:S(2)}) copy-start(s32[1,1024]{1,0:T(1,128)} %param.22) | copy-start | bytes 12292
  113.3 52.6 %copy-start.6 = (s32[1,1024]{1,0:T(1,128)S(1)}, s32[1,1024]{1,0:T(1,128)}, u32[]{:S(2)}) copy-start(s32[1,1024]{1,0:T(1,128)} %sr_ref.1) | copy-start | bytes 12292
  113.3 53.9 %copy-start = (s32[1024,1]{1,0:T(8,128)S(1)}, s32[1024,1]{1,0:T(8,128)}, u32[]{:S(2)}) copy-start(s32[1024,1]{1,0:T(8,128)} %copy.44.sc_ref) | copy-start | bytes 12292
  317.6 2.8 copy-start.3
  317.6 3.5 %copy-start.5 = (f32[48,768]{1,0:T(8,128)S(1)}, f32[48,768]{1,0:T(8,128)}, u32[]{:S(2)}) copy-start(f32[48,768]{1,0:T(8,128)} %get-tuple-element.124) | copy-start | bytes 442372
  317.6 4.2 %copy-start.2 = (f32[192,768]{1,0:T(8,128)S(1)}, f32[192,768]{1,0:T(8,128)}, u32[]{:S(2)}) copy-start(f32[192,768]{1,0:T(8,128)} %get-tuple-element.85) | copy-start | bytes 1769476
  320.4 2.3 copy-start.1
  320.4 3.1 copy-start.4

commit v5 on v4

--- a/solution.py
+++ b/solution.py
@@ -600,7 +600,7 @@
 
 
 def finish_and_reduce(pairs, tokens, resid_grad, vecs, qkv_t, sums, shard_rows, cuts, blocks, nz, collective, tile=256,
-                      qkv=2, first_tile=7, lags=(1, 2, 4, 6, 7)):
+                      qkv=2, first_tile=7, lags=(1, 3, 5, 7, 8)):
     nw = len(pairs)
     lefts = [a for ls, _ in pairs for a in ls]
     rights = [r for _, r in pairs]

time: 324 us -> 328 us (1.012)
  Pallas kernels: 301 us -> 305 us
    pallas_call x1, Pallas kernels: 109 us -> 113 us  [finish_and_reduce(): pl.pallas_call(kernel, out_shape=[jax.ShapeDtypeStruct((rw, width), F32)...]
where the time goes in v5:
time: 328 us
  Pallas kernels  305 us (93%)
  local copies, waits for them, and re-layouts  18 us (5%)
  other arithmetic  4.41 us (1%)
    pallas_call x1, Pallas kernels, finish_and_reduce(): pl.pallas_call(kernel, out_shape=[jax.ShapeDtypeStruct((rw, width), F32)...  113 us
    pallas_call x1, Pallas kernels, gather_attend(): pl.pallas_call(kernel, out_shape=[sds((n, d), BF16), sds((n, 3 * d), BF16...  103 us
    pallas_call x2, Pallas kernels, call(): pl.pallas_call(kernel, grid_spec=pltpu.PrefetchScalarGridSpec(num_scalar_...  89.5 us

profile of v5, /device:TPU:0, one launch (start us, length us, event | category | flops | bytes accessed | tf_op | source)
XLA Modules:
  0.0 328.1 jit_solution(17181058818145935972)
XLA Ops:
  0.7 1.7 copy.44.sc_ref
  2.4 0.7 slice_bitcast_fusion.8
  3.0 0.7 slice_bitcast_fusion.9
  3.7 1.4 pad_add_fusion.p_ref
  5.1 1.3 compare_select_fusion.kr_ref
  6.4 102.9 %gather_attend.1 = (bf16[1024,768]{1,0:T(8,128)(2,1)}, bf16[1024,2304]{1,0:T(8,128)(2,1)}, f32[8,768]{1,0:T(8,128)}, bf16[1024,768]{1,0:T(8,128)(2,1)}, f32[6,8,...) custom-call(bf16[1024,768]{1,0:T(8,128)(2,1)} %refs_12_.1, ...), custom_call_target="tpu_custom_call" | custom-call | tf_op jit(solution)/shard_map/gather_attend/pallas_call | solution.py:573
  109.3 0.8 slice.68
  110.1 0.7 reshape.266.ub_ref
  110.8 0.8 slice.70
  111.6 0.7 reshape.267.ab_ref
  112.2 1.0 copy.46.v_ref
  113.3 52.6 %middle.1 = (bf16[1024,768]{1,0:T(8,128)(2,1)}, bf16[1024,3072]{1,0:T(8,128)(2,1)}, bf16[1024,3072]{1,0:T(8,128)(2,1)}, bf16[1024,768]{1,0:T(8,128)(2,1)}, bf16[...) custom-call(bf16[1024,768]{1,0:T(8,128)(2,1)} %refs_12_.1, ...), custom_call_target="tpu_custom_call" | custom-call | tf_op jit(solution)/shard_map/middle/pallas_call | solution.py:58
  167.2 0.8 broadcast_select_fusion.kc_ref
  168.0 36.9 %attend_back.1 = (bf16[1024,768]{1,0:T(8,128)(2,1)}, bf16[1024,768]{1,0:T(8,128)(2,1)}, bf16[1024,768]{1,0:T(8,128)(2,1)}, f32[8,768]{1,0:T(8,128)}, f32[8,768]{1,0:T(8,128)}) custom-call(s32[2,4]{1,0:T(2,128)} %pad_add_fusion.1.win, bf16[1024,2304]{1,0:T(8,128)(2,1)} %get-tuple-element.63.q_ref.k_ref.v_ref, ...), custom_call_target="tpu_custom_call" | custom-call | tf_op jit(solution)/shard_map/attend_back/pallas_call | solution.py:58
  204.9 112.6 %finish_reduce.1 = (f32[64,768]{1,0:T(8,128)}, f32[192,768]{1,0:T(8,128)}, f32[144,768]{1,0:T(8,128)}, f32[192,768]{1,0:T(8,128)}, f32[48,768]{1,0:T(8,128)}, /*...) custom-call(bf16[1024,1024]{1,0:T(8,128)(2,1)} %refs_0_.1, bf16[1024,3072]{1,0:T(8,128)(2,1)} %get-tuple-element.62.refs_1_, ...), custom_call_target="tpu_custom_call" | custom-call | tf_op jit(solution)/shard_map/finish_reduce/pallas_call | solution.py:853
  317.5 0.8 slice.65
  318.9 0.8 constant_dynamic-slice_fusion
  320.2 0.8 slice.67
  321.6 2.7 copy.60
  324.4 0.8 copy.61
  325.1 0.7 copy.62
  325.8 0.8 copy.63
  326.6 0.8 copy.64
  327.4 0.7 copy.65
  (31 shorter events, 3.1 us)
Async XLA Ops:
  6.4 105.8 %copy-start.7 = (s32[1,1024]{1,0:T(1,128)S(1)}, s32[1,1024]{1,0:T(1,128)}, u32[]{:S(2)}) copy-start(s32[1,1024]{1,0:T(1,128)} %param.22) | copy-start | bytes 12292
  113.3 52.6 %copy-start.6 = (s32[1,1024]{1,0:T(1,128)S(1)}, s32[1,1024]{1,0:T(1,128)}, u32[]{:S(2)}) copy-start(s32[1,1024]{1,0:T(1,128)} %sr_ref.1) | copy-start | bytes 12292
  113.3 53.9 %copy-start = (s32[1024,1]{1,0:T(8,128)S(1)}, s32[1024,1]{1,0:T(8,128)}, u32[]{:S(2)}) copy-start(s32[1024,1]{1,0:T(8,128)} %copy.44.sc_ref) | copy-start | bytes 12292
  321.6 2.8 copy-start.3
  321.6 3.5 %copy-start.5 = (f32[48,768]{1,0:T(8,128)S(1)}, f32[48,768]{1,0:T(8,128)}, u32[]{:S(2)}) copy-start(f32[48,768]{1,0:T(8,128)} %get-tuple-element.124) | copy-start | bytes 442372
  321.6 4.2 %copy-start.2 = (f32[192,768]{1,0:T(8,128)S(1)}, f32[192,768]{1,0:T(8,128)}, u32[]{:S(2)}) copy-start(f32[192,768]{1,0:T(8,128)} %get-tuple-element.85) | copy-start | bytes 1769476
  324.3 2.3 copy-start.1
  324.3 3.1 copy-start.4
